TPU v7x, 32 devices: a whole 2x2x4 slice. The times are simulated.
32 devices in a mesh: seq: 4 (over y, x), fsdp: 8 (over z, core).
Axes of the slice: x: 2, y: 2, z: 4, core: 2. Of those that a mesh axis runs over, the one named last changes fastest.
Arguments:
- tokens: bfloat16 [8, 1024, 768], P('fsdp', 'seq'), may hold values from -6 to 6
- norm_gain: float32 [768], replicated, may hold values from 0.1 to 1.9
- in_weight: bfloat16 [768, 3328], P('fsdp'), may hold values from -0.21875 to 0.21875
- dt_weight: bfloat16 [768, 24], P('fsdp'), may hold values from -0.21875 to 0.21875
- conv_x_weight: float32 [4, 1536], replicated, may hold values from -3 to 3
- conv_x_bias: float32 [1536], replicated, may hold values from -0.5 to 0.5
- conv_bc_weight: float32 [4, 256], replicated, may hold values from -3 to 3
- conv_bc_bias: float32 [256], replicated, may hold values from -0.5 to 0.5
- dt_bias: float32 [24], replicated, may hold values from -7 to -3
- a_log: float32 [24], replicated, may hold values from 0 to 2.77
- d_skip: float32 [24], replicated, may hold values from 0.5 to 1.5
- gate_gain: float32 [1536], replicated, may hold values from 0.1 to 1.9
- out_weight: bfloat16 [1536, 768], P('fsdp'), may hold values from -0.15625 to 0.15625
- cotangent: bfloat16 [8, 1024, 768], P('fsdp', 'seq'), may hold values from -6 to 6
Outputs:
- result: float32 [8, 1024, 768], P('fsdp', 'seq')
- grad_tokens: float32 [8, 1024, 768], P('fsdp', 'seq')
- norm_gain_grad: float32 [768], replicated
- in_weight_grad: float32 [768, 3328], P('fsdp')
- dt_weight_grad: float32 [768, 24], P('fsdp')
- conv_x_weight_grad: float32 [4, 1536], replicated
- conv_x_bias_grad: float32 [1536], replicated
- conv_bc_weight_grad: float32 [4, 256], replicated
- conv_bc_bias_grad: float32 [256], replicated
- dt_bias_grad: float32 [24], replicated
- a_log_grad: float32 [24], replicated
- d_skip_grad: float32 [24], replicated
- gate_gain_grad: float32 [1536], replicated
- out_weight_grad: float32 [1536, 768], P('fsdp')
All inputs are finite; a program needn't handle non-finite values.
Results may differ from a plain program's by a relative error of at most 0.012.
The roundings to bfloat16 on the way count: a program that leaves them out, or rounds other values in their place, can miss the bound.
Values may be sent and summed in bfloat16 or wider, within the bound.
No kernel may reach another device: no remote copies, remote signals or barrier semaphores. Data moves between devices by JAX's collectives and lax.ppermute only.
A program may use at most 192 MiB of HBM per device.

v0:
```python
import jax
import jax.numpy as jnp
from jax import lax
from jax.sharding import PartitionSpec as P

SPAN = 256


EPSILON = 1e-05


def pre_norm(tok_float, gain_vec):
    scale_rows = lax.rsqrt(jnp.mean(tok_float * tok_float, axis=-1, keepdims=True) + EPSILON)
    return tok_float * scale_rows * gain_vec


def gate_norm(ssm_float, gate_float, gain_vec):
    gated = ssm_float * jax.nn.silu(gate_float)
    scale_rows = lax.rsqrt(jnp.mean(gated * gated, axis=-1, keepdims=True) + EPSILON)
    return gated * scale_rows * gain_vec


def causal_conv(values, tap_weights, offset):
    tap_count = tap_weights.shape[0]
    length = values.shape[0]
    padded = jnp.pad(values, ((tap_count - 1, 0), (0, 0)))
    summed = offset[None, :] + jnp.zeros_like(values)
    for tap_index in range(tap_count):
        summed = summed + tap_weights[tap_index][None, :] * padded[tap_index : tap_index + length]
    return jax.nn.silu(summed)


def block_scan(x_heads, b_rows, c_rows, step_sizes, decay_rate, block_size):
    length, head_count, head_dim = x_heads.shape
    state_size = b_rows.shape[1]
    block_count = length // block_size
    highest = lax.Precision.HIGHEST
    x_blocks = x_heads.reshape(block_count, block_size, head_count, head_dim)
    b_blocks = b_rows.reshape(block_count, block_size, state_size)
    c_blocks = c_rows.reshape(block_count, block_size, state_size)
    d_blocks = step_sizes.reshape(block_count, block_size, head_count).transpose(0, 2, 1)
    causal = jnp.arange(block_size)[:, None] >= jnp.arange(block_size)[None, :]

    def advance(carry_state, inputs):
        x_block, b_block, c_block, d_block = inputs
        decays = jnp.cumsum(d_block * decay_rate[:, None], axis=1)
        scores = jnp.dot(c_block, b_block.T, precision=highest)
        spread = decays[:, :, None] - decays[:, None, :]
        kernel = jnp.where(causal[None], jnp.exp(jnp.where(causal[None], spread, 0.0)), 0.0)
        kernel = kernel * scores[None] * d_block[:, None, :]
        within = jnp.einsum("hts,shp->thp", kernel, x_block, precision=highest)
        carried = jnp.einsum("tn,hpn->thp", c_block, carry_state, precision=highest)
        carried = carried * jnp.exp(decays).T[:, :, None]
        last_decay = decays[:, -1]
        weights_in = jnp.exp(last_decay[:, None] - decays) * d_block
        updated = carry_state * jnp.exp(last_decay)[:, None, None]
        updated = updated + jnp.einsum(
            "hs,shp,sn->hpn", weights_in, x_block, b_block, precision=highest
        )
        return (updated, within + carried)

    start_state = jnp.zeros((head_count, head_dim, state_size), jnp.float32)
    unused, outputs = lax.scan(advance, start_state, (x_blocks, b_blocks, c_blocks, d_blocks))
    return outputs.reshape(length, head_count, head_dim)


def mixer(
    x_input,
    dt_input,
    bc_input,
    conv_x_weight,
    conv_x_bias,
    conv_bc_weight,
    conv_bc_bias,
    dt_bias,
    a_log,
    d_skip,
):
    length, inner_width = x_input.shape
    head_count = dt_input.shape[1]
    head_dim = inner_width // head_count
    state_size = bc_input.shape[1] // 2
    x_conv = causal_conv(x_input, conv_x_weight, conv_x_bias)
    bc_conv = causal_conv(bc_input, conv_bc_weight, conv_bc_bias)
    step_sizes = jax.nn.softplus(dt_input + dt_bias[None, :])
    decay_rate = -jnp.exp(a_log)
    x_heads = x_conv.reshape(length, head_count, head_dim)
    outputs = block_scan(
        x_heads, bc_conv[:, :state_size], bc_conv[:, state_size:], step_sizes, decay_rate, SPAN
    )
    outputs = outputs + d_skip[None, :, None] * x_heads
    return outputs.reshape(length, inner_width)


def contract_rows(left, right):
    return lax.dot_general(
        left, right, (((0,), (0,)), ((), ())), preferred_element_type=jnp.float32
    )


def local(
    tokens,
    norm_gain,
    in_weight,
    dt_weight,
    conv_x_weight,
    conv_x_bias,
    conv_bc_weight,
    conv_bc_bias,
    dt_bias,
    a_log,
    d_skip,
    gate_gain,
    out_weight,
    cotangent,
):
    tok_rows = tokens[0]
    cot_rows = cotangent[0]
    inner_width = gate_gain.shape[0]
    proj_width = in_weight.shape[1]
    tok_float = tok_rows.astype(jnp.float32)
    normed_float, pre_back = jax.vjp(pre_norm, tok_float, norm_gain)
    normed = normed_float.astype(jnp.bfloat16)
    full_in, full_dt, full_out = (
        lax.all_gather(in_weight, "fsdp", axis=0, tiled=True),
        lax.all_gather(dt_weight, "fsdp", axis=0, tiled=True),
        lax.all_gather(out_weight, "fsdp", axis=0, tiled=True),
    )
    projected = jnp.dot(normed, full_in, preferred_element_type=jnp.float32).astype(jnp.bfloat16)
    dt_input = jnp.dot(normed, full_dt, preferred_element_type=jnp.float32).astype(jnp.bfloat16)
    gate_input = projected[:, :inner_width]
    x_input = projected[:, inner_width : 2 * inner_width]
    bc_input = projected[:, 2 * inner_width :]
    x_group, dt_group = (
        lax.all_to_all(x_input, "seq", split_axis=1, concat_axis=0, tiled=True),
        lax.all_to_all(dt_input, "seq", split_axis=1, concat_axis=0, tiled=True),
    )
    bc_whole = lax.all_gather(bc_input, "seq", axis=0, tiled=True)
    group = lax.axis_index("seq")
    group_count = lax.axis_size("seq")
    group_width = inner_width // group_count
    group_heads = dt_bias.shape[0] // group_count
    col_start = group * group_width
    head_start = group * group_heads
    local_params = (
        lax.dynamic_slice_in_dim(conv_x_weight, col_start, group_width, 1),
        lax.dynamic_slice_in_dim(conv_x_bias, col_start, group_width, 0),
        conv_bc_weight,
        conv_bc_bias,
        lax.dynamic_slice_in_dim(dt_bias, head_start, group_heads, 0),
        lax.dynamic_slice_in_dim(a_log, head_start, group_heads, 0),
        lax.dynamic_slice_in_dim(d_skip, head_start, group_heads, 0),
    )
    ssm_float, mixer_back = jax.vjp(
        mixer,
        x_group.astype(jnp.float32),
        dt_group.astype(jnp.float32),
        bc_whole.astype(jnp.float32),
        *local_params
    )
    ssm_out = lax.all_to_all(
        ssm_float.astype(jnp.bfloat16), "seq", split_axis=0, concat_axis=1, tiled=True
    )
    mixed_float, gate_back = jax.vjp(
        gate_norm, ssm_out.astype(jnp.float32), gate_input.astype(jnp.float32), gate_gain
    )
    mixed = mixed_float.astype(jnp.bfloat16)
    result = tok_float + jnp.dot(mixed, full_out, preferred_element_type=jnp.float32)
    back_in, back_dt, back_out = (
        lax.all_gather(in_weight, "fsdp", axis=0, tiled=True),
        lax.all_gather(dt_weight, "fsdp", axis=0, tiled=True),
        lax.all_gather(out_weight, "fsdp", axis=0, tiled=True),
    )
    grad_mixed = jnp.dot(cot_rows, back_out.T, preferred_element_type=jnp.float32)
    piece = mixed
    out_part = lax.psum_scatter(
        contract_rows(piece, cot_rows), "fsdp", scatter_dimension=0, tiled=True
    )
    grad_ssm, grad_gate, grad_gate_gain = gate_back(grad_mixed)
    grad_group = lax.all_to_all(
        grad_ssm.astype(jnp.bfloat16), "seq", split_axis=1, concat_axis=0, tiled=True
    )
    mixer_grads = mixer_back(grad_group.astype(jnp.float32))
    grad_x, grad_dt = (
        lax.all_to_all(
            mixer_grads[0].astype(jnp.bfloat16), "seq", split_axis=0, concat_axis=1, tiled=True
        ),
        lax.all_to_all(
            mixer_grads[1].astype(jnp.bfloat16), "seq", split_axis=0, concat_axis=1, tiled=True
        ),
    )
    grad_bc = lax.psum_scatter(mixer_grads[2], "seq", scatter_dimension=0, tiled=True).astype(
        jnp.bfloat16
    )
    grad_proj = jnp.concatenate([grad_gate.astype(jnp.bfloat16), grad_x, grad_bc], axis=1)
    grad_normed = jnp.dot(grad_proj, back_in.T, preferred_element_type=jnp.float32)
    grad_normed = grad_normed + jnp.dot(grad_dt, back_dt.T, preferred_element_type=jnp.float32)
    piece = normed
    in_part = lax.psum_scatter(
        jnp.concatenate([contract_rows(piece, grad_proj), contract_rows(piece, grad_dt)], axis=1),
        "fsdp",
        scatter_dimension=0,
        tiled=True,
    )
    grad_tok, grad_norm_gain = pre_back(grad_normed)
    grad_tokens = cot_rows.astype(jnp.float32) + grad_tok
    in_total, out_weight_grad = lax.psum((in_part, out_part), "seq")
    in_weight_grad = in_total[:, :proj_width]
    dt_weight_grad = in_total[:, proj_width:]
    conv_x_full = lax.dynamic_update_slice_in_dim(
        jnp.zeros(conv_x_weight.shape, jnp.float32), mixer_grads[3], col_start, 1
    )
    conv_xb_full = lax.dynamic_update_slice_in_dim(
        jnp.zeros(conv_x_bias.shape, jnp.float32), mixer_grads[4], col_start, 0
    )
    dt_bias_full = lax.dynamic_update_slice_in_dim(
        jnp.zeros(dt_bias.shape, jnp.float32), mixer_grads[7], head_start, 0
    )
    a_log_full = lax.dynamic_update_slice_in_dim(
        jnp.zeros(a_log.shape, jnp.float32), mixer_grads[8], head_start, 0
    )
    d_skip_full = lax.dynamic_update_slice_in_dim(
        jnp.zeros(d_skip.shape, jnp.float32), mixer_grads[9], head_start, 0
    )
    small_totals = lax.psum(
        (
            grad_norm_gain,
            grad_gate_gain,
            conv_x_full,
            conv_xb_full,
            mixer_grads[5],
            mixer_grads[6],
            dt_bias_full,
            a_log_full,
            d_skip_full,
        ),
        ("seq", "fsdp"),
    )
    (
        norm_gain_grad,
        gate_gain_grad,
        conv_x_weight_grad,
        conv_x_bias_grad,
        conv_bc_weight_grad,
        conv_bc_bias_grad,
        dt_bias_grad,
        a_log_grad,
        d_skip_grad,
    ) = small_totals
    return (
        result[None],
        grad_tokens[None],
        norm_gain_grad,
        in_weight_grad,
        dt_weight_grad,
        conv_x_weight_grad,
        conv_x_bias_grad,
        conv_bc_weight_grad,
        conv_bc_bias_grad,
        dt_bias_grad,
        a_log_grad,
        d_skip_grad,
        gate_gain_grad,
        out_weight_grad,
    )


def solution(mesh):
    placed = (
        P("fsdp", "seq", None),
        P(),
        P("fsdp", None),
        P("fsdp", None),
        P(),
        P(),
        P(),
        P(),
        P(),
        P(),
        P(),
        P(),
        P("fsdp", None),
        P("fsdp", "seq", None),
    )
    return jax.shard_map(
        local,
        mesh=mesh,
        in_specs=placed,
        out_specs=(
            P("fsdp", "seq", None),
            P("fsdp", "seq", None),
            P(),
            P("fsdp", None),
            P("fsdp", None),
            P(),
            P(),
            P(),
            P(),
            P(),
            P(),
            P(),
            P(),
            P("fsdp", None),
        ),
        check_vma=False,
    )
```

profile of v0, /device:TPU:0, one launch (start us, length us, event | category | flops | bytes accessed | tf_op | source)
XLA Modules:
  0.0 729.6 jit_solution(13573644344247943185)
XLA Ops:
  8.0 16.0 %all-gather = bf16[8,96,24]{1,2,0:T(8,128)(2,1)S(1)} all-gather(bf16[1,96,24]{1,2,0:T(8,128)(2,1)} %bitcast.593), channel_id=1, replica_groups=mesh['seq'=4,'fsdp'=8] {'fsdp'}, dimensions={0}, use_global_device_ids=true | all-gather | bytes 41472 | tf_op jit(solution)/shard_map/all_gather | solution.py:126
  36.3 31.0 %all-gather.4.cloned.1.call-done = bf16[768,3328]{1,0:T(8,128)(2,1)} async-done(((bf16[96,3328]{1,0:T(8,128)(2,1)}), bf16[768,3328]{1,0:T(8,128)(2,1)}) %all-gather.4.cloned.1.call-update) | async-done | bytes 5111824 | tf_op jit(solution)/shard_map/all_gather | solution.py:125
  76.6 17.2 %all_gather.17 = bf16[1024,256]{1,0:T(8,128)(2,1)S(1)} all-gather(bf16[256,256]{1,0:T(8,128)(2,1)S(1)} %slice-done), channel_id=1, replica_groups=mesh['seq'=4,'fsdp'=8] {'seq'}, dimensions={0}, use_global_device_ids=true | all-gather | bytes 655360 | tf_op jit(solution)/shard_map/all_gather | solution.py:138
  107.8 114.5 %while.75 = (s32[]{:T(128)}, f32[6,64,128]{2,1,0:T(8,128)S(1)}, f32[4,256,6,64]{1,0,3,2:T(4,128)}, f32[4,128,256]{1,2,0:T(8,128)}, f32[4,6,256,256]{3,2,1,0:T(8,...) while((s32[]{:T(128)}, f32[6,64,128]{2,1,0:T(8,128)S(1)}, ...), condition=%wide.region_4.5_spmd.clone.clone, body=%wide.region_1.4_spmd.clone.clone.sunk | while | flops 709420032 | bytes 14227041 | solution.py:63
  119.7 9.5 %dynamic_update_slice.261 = f32[4,256,6,64]{1,0,3,2:T(4,128)} dynamic-update-slice(f32[4,256,6,64]{1,0,3,2:T(4,128)} %get-tuple-element.2225, f32[1,256,6,64]{1,0,3,2:T(1,128)S(1)} %copy.248, s32[]{:T(128)} %get-tuple-element.2223, s32[]{:T(128)} %constant.189.clone.1..sunk, s32[]{:T(128)} %constant.189.clone.1..sunk, s32[]{:T(128)} %constant.189.clone.1..sunk) | dynamic-update-slice | bytes 786436 | tf_op jit(solution)/shard_map/jvp()/while/body/jit(dynamic_update_index_in_dim)/dynamic_update_slice | solution.py:63
  148.4 9.5 %dynamic_update_slice.261 = f32[4,256,6,64]{1,0,3,2:T(4,128)} dynamic-update-slice(f32[4,256,6,64]{1,0,3,2:T(4,128)} %get-tuple-element.2225, f32[1,256,6,64]{1,0,3,2:T(1,128)S(1)} %copy.248, s32[]{:T(128)} %get-tuple-element.2223, s32[]{:T(128)} %constant.189.clone.1..sunk, s32[]{:T(128)} %constant.189.clone.1..sunk, s32[]{:T(128)} %constant.189.clone.1..sunk) | dynamic-update-slice | bytes 786436 | tf_op jit(solution)/shard_map/jvp()/while/body/jit(dynamic_update_index_in_dim)/dynamic_update_slice | solution.py:63
  177.0 9.5 %dynamic_update_slice.261 = f32[4,256,6,64]{1,0,3,2:T(4,128)} dynamic-update-slice(f32[4,256,6,64]{1,0,3,2:T(4,128)} %get-tuple-element.2225, f32[1,256,6,64]{1,0,3,2:T(1,128)S(1)} %copy.248, s32[]{:T(128)} %get-tuple-element.2223, s32[]{:T(128)} %constant.189.clone.1..sunk, s32[]{:T(128)} %constant.189.clone.1..sunk, s32[]{:T(128)} %constant.189.clone.1..sunk) | dynamic-update-slice | bytes 786436 | tf_op jit(solution)/shard_map/jvp()/while/body/jit(dynamic_update_index_in_dim)/dynamic_update_slice | solution.py:63
  205.7 9.5 %dynamic_update_slice.261 = f32[4,256,6,64]{1,0,3,2:T(4,128)} dynamic-update-slice(f32[4,256,6,64]{1,0,3,2:T(4,128)} %get-tuple-element.2225, f32[1,256,6,64]{1,0,3,2:T(1,128)S(1)} %copy.248, s32[]{:T(128)} %get-tuple-element.2223, s32[]{:T(128)} %constant.189.clone.1..sunk, s32[]{:T(128)} %constant.189.clone.1..sunk, s32[]{:T(128)} %constant.189.clone.1..sunk) | dynamic-update-slice | bytes 786436 | tf_op jit(solution)/shard_map/jvp()/while/body/jit(dynamic_update_index_in_dim)/dynamic_update_slice | solution.py:63
  228.3 13.4 %all_to_all.87 = bf16[4,256,384]{2,1,0:T(8,128)(2,1)S(1)} all-to-all(bf16[4,256,384]{2,1,0:T(8,128)(2,1)S(1)} %bitcast.567), channel_id=1, replica_groups=mesh['seq'=4,'fsdp'=8] {'seq'}, dimensions={0} | all-to-all | bytes 1572864 | tf_op jit(solution)/shard_map/all_to_all | solution.py:161
  255.1 8.7 %all-to-all-done.3 = bf16[256,4,384]{2,0,1:T(8,128)(2,1)S(1)} async-done(((bf16[256,4,384]{2,0,1:T(8,128)(2,1)}), bf16[256,4,384]{2,0,1:T(8,128)(2,1)S(1)}, u32[]{:S(2)}, u32[]{:S(2)}) %all-to-all-start.3) | async-done | bytes 786464 | tf_op jit(solution)/shard_map/all_to_all | solution.py:180
  271.5 176.0 %while.76 = (s32[]{:T(128)}, f32[6]{0:T(128)S(1)}, f32[6,64,128]{2,1,0:T(8,128)S(1)}, f32[4,256,6,64]{1,0,3,2:T(4,128)}, f32[4,256,128]{2,1,0:T(8,128)}, /*index...) while((s32[]{:T(128)}, f32[6]{0:T(128)S(1)}, ...), condition=%wide.region_18.19_spmd.clone.clone, body=%wide.region_7.18_spmd.clone.clone.sunk | while | flops 1415007744 | bytes 20314508 | solution.py:63
  277.4 9.5 %dynamic_update_slice.266 = f32[4,256,6,64]{1,0,3,2:T(4,128)} dynamic-update-slice(f32[4,256,6,64]{1,0,3,2:T(4,128)} %get-tuple-element.2316, f32[1,256,6,64]{1,0,3,2:T(1,128)} %copy.256, s32[]{:T(128)S(6)} %sub.236, s32[]{:T(128)} %constant.189.clone.1..sunk.1, s32[]{:T(128)} %constant.189.clone.1..sunk.1, s32[]{:T(128)} %constant.189.clone.1..sunk.1) | dynamic-update-slice | bytes 786436 | tf_op jit(solution)/shard_map/transpose(jvp())/while/body/jit(dynamic_update_index_in_dim)/dynamic_update_slice | solution.py:63
  290.8 5.4 fusion.261
  298.1 7.6 %reduce-window.50 = f32[6,2,128]{2,1,0:T(2,128)S(1)} reduce-window(f32[6,2,128]{2,1,0:T(2,128)S(1)} %reshape.634, f32[]{:T(128)} %constant.190.clone.1..sunk.1), window={size=1x1x128 pad=0_0x0_0x0_127}, to_apply=%region_13.13 | reduce-window | flops 195072 | bytes 12292 | tf_op jit(solution)/shard_map/reduce-window.18
  321.5 9.5 %dynamic_update_slice.266 = f32[4,256,6,64]{1,0,3,2:T(4,128)} dynamic-update-slice(f32[4,256,6,64]{1,0,3,2:T(4,128)} %get-tuple-element.2316, f32[1,256,6,64]{1,0,3,2:T(1,128)} %copy.256, s32[]{:T(128)S(6)} %sub.236, s32[]{:T(128)} %constant.189.clone.1..sunk.1, s32[]{:T(128)} %constant.189.clone.1..sunk.1, s32[]{:T(128)} %constant.189.clone.1..sunk.1) | dynamic-update-slice | bytes 786436 | tf_op jit(solution)/shard_map/transpose(jvp())/while/body/jit(dynamic_update_index_in_dim)/dynamic_update_slice | solution.py:63
  334.8 5.4 fusion.261
  342.1 7.6 %reduce-window.50 = f32[6,2,128]{2,1,0:T(2,128)S(1)} reduce-window(f32[6,2,128]{2,1,0:T(2,128)S(1)} %reshape.634, f32[]{:T(128)} %constant.190.clone.1..sunk.1), window={size=1x1x128 pad=0_0x0_0x0_127}, to_apply=%region_13.13 | reduce-window | flops 195072 | bytes 12292 | tf_op jit(solution)/shard_map/reduce-window.18
  365.4 9.5 %dynamic_update_slice.266 = f32[4,256,6,64]{1,0,3,2:T(4,128)} dynamic-update-slice(f32[4,256,6,64]{1,0,3,2:T(4,128)} %get-tuple-element.2316, f32[1,256,6,64]{1,0,3,2:T(1,128)} %copy.256, s32[]{:T(128)S(6)} %sub.236, s32[]{:T(128)} %constant.189.clone.1..sunk.1, s32[]{:T(128)} %constant.189.clone.1..sunk.1, s32[]{:T(128)} %constant.189.clone.1..sunk.1) | dynamic-update-slice | bytes 786436 | tf_op jit(solution)/shard_map/transpose(jvp())/while/body/jit(dynamic_update_index_in_dim)/dynamic_update_slice | solution.py:63
  378.8 5.4 fusion.261
  386.1 7.6 %reduce-window.50 = f32[6,2,128]{2,1,0:T(2,128)S(1)} reduce-window(f32[6,2,128]{2,1,0:T(2,128)S(1)} %reshape.634, f32[]{:T(128)} %constant.190.clone.1..sunk.1), window={size=1x1x128 pad=0_0x0_0x0_127}, to_apply=%region_13.13 | reduce-window | flops 195072 | bytes 12292 | tf_op jit(solution)/shard_map/reduce-window.18
  409.5 9.5 %dynamic_update_slice.266 = f32[4,256,6,64]{1,0,3,2:T(4,128)} dynamic-update-slice(f32[4,256,6,64]{1,0,3,2:T(4,128)} %get-tuple-element.2316, f32[1,256,6,64]{1,0,3,2:T(1,128)} %copy.256, s32[]{:T(128)S(6)} %sub.236, s32[]{:T(128)} %constant.189.clone.1..sunk.1, s32[]{:T(128)} %constant.189.clone.1..sunk.1, s32[]{:T(128)} %constant.189.clone.1..sunk.1) | dynamic-update-slice | bytes 786436 | tf_op jit(solution)/shard_map/transpose(jvp())/while/body/jit(dynamic_update_index_in_dim)/dynamic_update_slice | solution.py:63
  422.9 5.4 fusion.261
  430.1 7.6 %reduce-window.50 = f32[6,2,128]{2,1,0:T(2,128)S(1)} reduce-window(f32[6,2,128]{2,1,0:T(2,128)S(1)} %reshape.634, f32[]{:T(128)} %constant.190.clone.1..sunk.1), window={size=1x1x128 pad=0_0x0_0x0_127}, to_apply=%region_13.13 | reduce-window | flops 195072 | bytes 12292 | tf_op jit(solution)/shard_map/reduce-window.18
  469.2 5.5 multiply_reduce_fusion.3
  476.5 4.3 all-to-all-start.4
  483.2 5.6 all-to-all-done.4
  493.8 4.7 pad_maximum_fusion
  498.6 38.4 %reduce-scatter.8.cloned.1.call-done = f32[192,768]{1,0:T(8,128)} async-done(((f32[1536,768]{1,0:T(8,128)}), f32[192,768]{1,0:T(8,128)}) %reduce-scatter.8.cloned.1.call-update) | async-done | bytes 589840 | tf_op jit(solution)/shard_map/reduce_scatter | solution.py:176
  537.0 111.2 %reduce-scatter.6.cloned.1.call-done = f32[96,3352]{1,0:T(8,128)} async-done(((f32[768,3352]{1,0:T(8,128)}), f32[96,3352]{1,0:T(8,128)}) %reduce-scatter.6.cloned.1.call-update) | async-done | bytes 1287184 | tf_op jit(solution)/shard_map/reduce_scatter | solution.py:199
  653.2 4.8 fusion.166
  658.8 39.1 %all-reduce.21 = (f32[768]{0:T(1024)}, f32[4,1536]{1,0:T(4,128)}, f32[1536]{0:T(1024)}, f32[4,256]{1,0:T(4,128)}, f32[256]{0:T(256)}, /*index=5*/f32[24]{0:T(128)}, f32[24]{0:T(128)}, f32[24]{0:T(128)}, f32[1536]{0:T(1024)}) all-reduce(f32[768]{0:T(1024)S(1)} %get-tuple-element.1640, ...), channel_id=1, replica_groups=mesh['seq'=4,'fsdp'=8] {'seq','fsdp'}, use_global_device_ids=true, to_apply=%region_22.23 | all-reduce | flops 11336 | bytes 90688 | tf_op jit(solution)/shard_map/psum | solution.py:225
  699.1 18.6 %all-reduce.25.cloned.1.call-done = (f32[96,3352]{1,0:T(8,128)}, f32[192,768]{1,0:T(8,128)}) async-done(((f32[96,3352]{1,0:T(8,128)}, f32[192,768]{1,0:T(8,128)}), (f32[96,3352]{1,0:T(8,128)}, f32[192,768]{1,0:T(8,128)})) %all-reduce.25.cloned.1.call-update) | async-done | bytes 1877008 | tf_op jit(solution)/shard_map/psum | solution.py:207
  (550 shorter events, 266.9 us)
Async XLA Ops:
  7.2 60.2 %copy-start.7 = (bf16[1,256,768]{2,1,0:T(8,128)(2,1)S(1)}, bf16[1,256,768]{2,1,0:T(8,128)(2,1)}, u32[]{:S(2)}) copy-start(bf16[1,256,768]{2,1,0:T(8,128)(2,1)} %param.18) | copy-start | bytes 1179652
  7.2 60.2 %copy-start.31 = (f32[768]{0:T(1024)S(1)}, f32[768]{0:T(1024)}, u32[]{:S(2)}) copy-start(f32[768]{0:T(1024)} %param.19) | copy-start | bytes 9220
  7.2 25.1 %copy-start.78 = (f32[4,256]{1,0:T(4,128)S(1)}, f32[4,256]{1,0:T(4,128)}, u32[]{:S(2)}) copy-start(f32[4,256]{1,0:T(4,128)} %param.24) | copy-start | bytes 12292
  7.2 25.2 %copy-start.82 = (f32[24]{0:T(128)S(1)}, f32[24]{0:T(128)}, u32[]{:S(2)}) copy-start(f32[24]{0:T(128)} %param.27) | copy-start | bytes 292
  7.2 25.3 %copy-start.84 = (f32[24]{0:T(128)S(1)}, f32[24]{0:T(128)}, u32[]{:S(2)}) copy-start(f32[24]{0:T(128)} %param.26) | copy-start | bytes 292
  7.2 25.4 %copy-start.85 = (f32[24]{0:T(128)S(1)}, f32[24]{0:T(128)}, u32[]{:S(2)}) copy-start(f32[24]{0:T(128)} %param.28) | copy-start | bytes 292
  7.2 60.1 %all-gather.4.cloned.1.call-start = ((), (), s32[]{:S(2)}) async-start(), calls=%async_computation.9 | async-start | bytes 5750784 | tf_op jit(solution)/shard_map/all_gather | solution.py:125
  27.8 8.4 %all-to-all-start = ((bf16[256,4,6]{0,2,1:T(8,128)(2,1)}), bf16[256,4,6]{0,2,1:T(8,128)(2,1)S(1)}, u32[]{:S(2)}, u32[]{:S(2)}) async-start(bf16[256,4,6]{0,2,1:T(8,128)(2,1)} %all_to_all.66), calls=%async_computation | async-start | bytes 32768 | tf_op jit(solution)/shard_map/all_to_all | solution.py:136
  31.5 213.6 %all-gather.6.cloned.1.call-start = ((), (), s32[]{:S(2)}) async-start(), calls=%async_computation.10 | async-start | bytes 2654208 | tf_op jit(solution)/shard_map/all_gather | solution.py:127
  32.3 62.3 %copy-start.55 = (f32[1,256]{1,0:T(1,128)}, f32[1,256]{1,0:T(1,128)S(1)}, u32[]{:S(2)}) copy-start(f32[1,256]{1,0:T(1,128)S(1)} %get-tuple-element.1809) | copy-start | bytes 3076
  32.3 62.3 %copy-start.57 = (f32[1,256]{1,0:T(1,128)}, f32[1,256]{1,0:T(1,128)S(1)}, u32[]{:S(2)}) copy-start(f32[1,256]{1,0:T(1,128)S(1)} %get-tuple-element.1810) | copy-start | bytes 3076
  32.4 62.3 %copy-start.59 = (f32[1,256]{1,0:T(1,128)}, f32[1,256]{1,0:T(1,128)S(1)}, u32[]{:S(2)}) copy-start(f32[1,256]{1,0:T(1,128)S(1)} %get-tuple-element.1811) | copy-start | bytes 3076
  32.4 62.3 %copy-start.61 = (f32[1,256]{1,0:T(1,128)}, f32[1,256]{1,0:T(1,128)S(1)}, u32[]{:S(2)}) copy-start(f32[1,256]{1,0:T(1,128)S(1)} %get-tuple-element.1812) | copy-start | bytes 3076
  32.7 38.7 %copy-start.79 = (f32[6]{0:T(128)}, f32[6]{0:T(128)S(1)}, u32[]{:S(2)}) copy-start(f32[6]{0:T(128)S(1)} %dynamic_slice.260) | copy-start | bytes 76
  32.9 195.2 %copy-start.54 = (f32[384]{0:T(512)}, f32[384]{0:T(512)S(1)}, u32[]{:S(2)}) copy-start(f32[384]{0:T(512)S(1)} %mul.816) | copy-start | bytes 4612
  34.6 63.6 %copy-start.44 = (f32[384]{0:T(512)}, f32[384]{0:T(512)S(1)}, u32[]{:S(2)}) copy-start(f32[384]{0:T(512)S(1)} %get-tuple-element.1644) | copy-start | bytes 4612
  34.6 63.5 %copy-start.46 = (f32[384]{0:T(512)}, f32[384]{0:T(512)S(1)}, u32[]{:S(2)}) copy-start(f32[384]{0:T(512)S(1)} %get-tuple-element.1645) | copy-start | bytes 4612
  34.6 63.5 %copy-start.48 = (f32[384]{0:T(512)}, f32[384]{0:T(512)S(1)}, u32[]{:S(2)}) copy-start(f32[384]{0:T(512)S(1)} %get-tuple-element.1646) | copy-start | bytes 4612
  34.6 63.5 %copy-start.50 = (f32[384]{0:T(512)}, f32[384]{0:T(512)S(1)}, u32[]{:S(2)}) copy-start(f32[384]{0:T(512)S(1)} %get-tuple-element.1647) | copy-start | bytes 4612
  36.3 35.1 %copy-start.34 = (bf16[256,4,6]{0,2,1:T(8,128)(2,1)}, bf16[256,4,6]{0,2,1:T(8,128)(2,1)S(1)}, u32[]{:S(2)}) copy-start(bf16[256,4,6]{0,2,1:T(8,128)(2,1)S(1)} %all-to-all-done) | copy-start | bytes 36868
  72.8 21.9 %copy-start.80 = (f32[256]{0:T(256)S(1)}, f32[256]{0:T(256)}, u32[]{:S(2)}) copy-start(f32[256]{0:T(256)} %param.25) | copy-start | bytes 3076
  72.8 24.4 %all-to-all-start.1 = ((bf16[256,4,384]{2,0,1:T(8,128)(2,1)}), bf16[256,4,384]{2,0,1:T(8,128)(2,1)S(1)}, u32[]{:S(2)}, u32[]{:S(2)}) async-start(bf16[256,4,384]{2,0,1:T(8,128)(2,1)} %bitcast.401), calls=%async_computation.1 | async-start | bytes 1572864 | tf_op jit(solution)/shard_map/all_to_all | solution.py:135
  251.5 12.3 %all-to-all-start.3 = ((bf16[256,4,384]{2,0,1:T(8,128)(2,1)}), bf16[256,4,384]{2,0,1:T(8,128)(2,1)S(1)}, u32[]{:S(2)}, u32[]{:S(2)}) async-start(bf16[256,4,384]{2,0,1:T(8,128)(2,1)} %bitcast.400), calls=%async_computation.3 | async-start | bytes 1572864 | tf_op jit(solution)/shard_map/all_to_all | solution.py:180
  255.0 234.7 %reduce-scatter.4.cloned.1.call-start = ((), (), s32[]{:S(2)}) async-start(), calls=%async_computation.11 | async-start | bytes 1310720 | tf_op jit(solution)/shard_map/reduce_scatter | solution.py:192
  453.5 83.5 %reduce-scatter.8.cloned.1.call-start = ((), (), s32[]{:S(2)}) async-start(), calls=%async_computation.13 | async-start | bytes 5308416 | tf_op jit(solution)/shard_map/reduce_scatter | solution.py:176
  460.0 9.2 %copy-start.4 = (f32[1024,384]{1,0:T(8,128)S(1)}, f32[1024,384]{1,0:T(8,128)}, u32[]{:S(2)}) copy-start(f32[1024,384]{1,0:T(8,128)} %copy-done.2) | copy-start | bytes 4718596
  465.2 11.2 %all-to-all-start.5 = ((bf16[4,256,6]{1,2,0:T(8,128)(2,1)}), bf16[4,256,6]{1,2,0:T(8,128)(2,1)}, u32[]{:S(2)}, u32[]{:S(2)}) async-start(bf16[4,256,6]{1,2,0:T(8,128)(2,1)} %get-tuple-element.1772), calls=%async_computation.6 | async-start | bytes 32768 | tf_op jit(solution)/shard_map/all_to_all | solution.py:188
  476.5 12.3 %all-to-all-start.4 = ((bf16[4,256,384]{2,1,0:T(8,128)(2,1)}), bf16[4,256,384]{2,1,0:T(8,128)(2,1)S(1)}, u32[]{:S(2)}, u32[]{:S(2)}) async-start(bf16[4,256,384]{2,1,0:T(8,128)(2,1)} %bitcast.22), calls=%async_computation.4 | async-start | bytes 1572864 | tf_op jit(solution)/shard_map/all_to_all | solution.py:185
  480.7 167.5 %reduce-scatter.6.cloned.1.call-start = ((), (), s32[]{:S(2)}) async-start(), calls=%async_computation.12 | async-start | bytes 11943936 | tf_op jit(solution)/shard_map/reduce_scatter | solution.py:199
  498.5 149.8 %copy-start.40 = (f32[256]{0:T(256)S(1)}, f32[256]{0:T(256)}, u32[]{:S(2)}) copy-start(f32[256]{0:T(256)} %fusion.189) | copy-start | bytes 3076
  498.6 219.2 %all-reduce.25.cloned.1.call-start = ((), (), s32[]{:S(2)}) async-start(), calls=%async_computation.14 | async-start | bytes 3833856 | tf_op jit(solution)/shard_map/psum | solution.py:207
  658.1 39.8 %copy-start.64 = (f32[256]{0:T(256)S(1)}, f32[256]{0:T(256)}, u32[]{:S(2)}) copy-start(f32[256]{0:T(256)} %copy-done.63) | copy-start | bytes 3076
  (72 other events, 277.1 us)
Sparse Core Ops, SparseCore 0:
  9.7 57.6 all-gather.3
  69.0 30.2 all-gather.5
  453.7 25.6 reduce-scatter.3
  481.5 55.4 reduce-scatter.7
  539.2 109.0 reduce-scatter.5
  651.4 66.2 all-reduce.24
where the time goes:
time: 737 us; the launch traced here: 730 us
  waiting for transfers between devices  217 us (29%)
  local copies, waits for them, and re-layouts  167 us (23%)
  matrix products  119 us (16%)
  other arithmetic  106 us (14%)
  blocking collectives  85.7 us (12%)
  starting transfers between devices  19.4 us (3%)
  between operations  15.5 us (2%)
    reduce_scatter x1, waiting for transfers between devices, local(): lax.psum_scatter(jnp.concatenate([contract_rows(piece, grad_proj), contra...  111 us
    dynamic_update_slice x36, local copies, waits for them, and re-layouts, block_scan(): lax.scan(advance, start_state, (x_blocks, b_blocks, c_blocks, d_blocks))  101 us
    dot_general x12, matrix products, advance(): within = jnp.einsum('hts,shp->thp', kernel, x_block, precision=highest)  39.5 us
    another operation x29, other arithmetic  39.4 us
    psum x1, blocking collectives, local(): lax.psum((grad_norm_gain, grad_gate_gain, conv_x_full, conv_xb_full, mixe...  39.1 us
    reduce_scatter x1, waiting for transfers between devices, local(): lax.psum_scatter(contract_rows(piece, cot_rows), 'fsdp', scatter_dimensio...  38.4 us
    all_gather x1, waiting for transfers between devices, local(): lax.all_gather(in_weight, 'fsdp', axis=0, tiled=True)  31 us
    dynamic_update_slice x20, other arithmetic, block_scan(): lax.scan(advance, start_state, (x_blocks, b_blocks, c_blocks, d_blocks))  21.9 us
  transfers between devices with their start and end apart: 11, of which 7 were waited for; matrix products, arithmetic and copies ran while one was open for 25% of the time, Pallas kernels for 0%

commit v1 on v0

v1 whole, which is shorter than its diff:
```python
import functools

import jax
import jax.numpy as jnp
from jax import lax
from jax.experimental import pallas as pl
from jax.experimental.pallas import tpu as pltpu
from jax.sharding import PartitionSpec as P

EPSILON = 1e-05
LANES = 128
CHUNK = 128
PAD = 8
F32 = jnp.float32
BF16 = jnp.bfloat16
VMEM_LIMIT = 60 * 1024 * 1024


def mm(left, right, dims):
    return lax.dot_general(left, right, (dims, ((), ())), preferred_element_type=F32)


def mm_nn(left, right):
    return mm(left, right, ((1,), (0,)))


def mm_nt(left, right):
    return mm(left, right, ((1,), (1,)))


def mm_tn(left, right):
    return mm(left, right, ((0,), (0,)))


def mm_exact(left, right):
    return jnp.dot(left, right, precision=lax.Precision.HIGHEST, preferred_element_type=F32)


def iota(shape, axis):
    return lax.broadcasted_iota(jnp.int32, shape, axis)


def spread_heads(cols, head_count, head_dim):
    rows = cols.shape[0]
    per_tile = LANES // head_dim
    lane = iota((rows, LANES), 1)
    tiles = []
    for tile in range(head_count // per_tile):
        value = jnp.broadcast_to(cols[:, tile * per_tile : tile * per_tile + 1], (rows, LANES))
        for extra in range(1, per_tile):
            head = tile * per_tile + extra
            other = jnp.broadcast_to(cols[:, head : head + 1], (rows, LANES))
            value = jnp.where(lane >= extra * head_dim, other, value)
        tiles.append(value)
    return jnp.concatenate(tiles, axis=1)


def split_heads(tile, head_dim):
    lane = iota(tile.shape, 1)
    zero = jnp.zeros_like(tile)
    return jnp.concatenate(
        [
            jnp.where((lane >= part * head_dim) & (lane < (part + 1) * head_dim), tile, zero)
            for part in range(LANES // head_dim)
        ],
        axis=0,
    )


def conv_pre(padded_rows, taps):
    count = 4
    rows = padded_rows.shape[0] - PAD
    total = jnp.broadcast_to(taps[count : count + 1], (rows, padded_rows.shape[1]))
    for tap in range(count):
        start = PAD - (count - 1) + tap
        total = total + taps[tap : tap + 1] * padded_rows[start : start + rows]
    return total


def sigmoid(value):
    return 1.0 / (1.0 + jnp.exp(-value))


def softplus(value):
    return jnp.maximum(value, 0.0) + jnp.log1p(jnp.exp(-jnp.abs(value)))


def decay_terms(dt_rows, heads, tril):
    raw = dt_rows + heads[0:1]
    step = softplus(raw)
    decay = mm_exact(tril, step * heads[1:2])
    return raw, step, decay


def proj_columns(proj_ref, width, bc_width):
    return (
        proj_ref.at[:, width : 2 * width],
        proj_ref.at[:, 2 * width : 2 * width + bc_width],
        proj_ref.at[:, 2 * width + bc_width :],
    )


def forward_kernel(
    head_dim, proj_ref, xt_ref, bt_ref, heads_ref, y_ref, save_ref, xpad, bpad, state
):
    length, width = y_ref.shape
    x_ref, bc_ref, dt_ref = proj_columns(proj_ref, width, bt_ref.shape[1])
    head_count = width // head_dim
    per_tile = LANES // head_dim
    xpad[0:PAD] = jnp.zeros((PAD, width), F32)
    bpad[0:PAD] = jnp.zeros((PAD, bc_ref.shape[1]), F32)
    xpad[PAD:] = x_ref[...].astype(F32)
    bpad[PAD:] = bc_ref[...].astype(F32)
    state[...] = jnp.zeros_like(state)
    row = iota((CHUNK, CHUNK), 0)
    col = iota((CHUNK, CHUNK), 1)
    causal = row >= col
    tril = causal.astype(F32)
    state_size = bc_ref.shape[1] // 2

    def chunk_step(chunk, unused):
        start = pl.multiple_of(chunk * CHUNK, CHUNK)
        u_x = conv_pre(xpad[pl.ds(start, CHUNK + PAD), :], xt_ref[...])
        x = u_x * sigmoid(u_x)
        u_b = conv_pre(bpad[pl.ds(start, CHUNK + PAD), :], bt_ref[...])
        bc = (u_b * sigmoid(u_b)).astype(BF16)
        b, c = bc[:, :state_size], bc[:, state_size:]
        raw, step, decay = decay_terms(
            dt_ref[pl.ds(start, CHUNK), :].astype(F32), heads_ref[...], tril
        )
        decay_t = jnp.transpose(decay)
        step_t = jnp.transpose(step)
        scores = mm_nt(c, b)
        xb = x.astype(BF16)
        within = []
        for tile in range(width // LANES):
            mats = []
            for part in range(per_tile):
                head = tile * per_tile + part
                gap = decay[:, head : head + 1] - decay_t[head : head + 1, :]
                fade = jnp.exp(jnp.where(causal, gap, -1e30))
                mats.append((fade * scores * step_t[head : head + 1, :]).astype(BF16))
            within.append(
                mm_nn(
                    jnp.concatenate(mats, axis=1),
                    split_heads(xb[:, tile * LANES : (tile + 1) * LANES], head_dim),
                )
            )
        within = jnp.concatenate(within, axis=1)
        old = state[...]
        old_b = old.astype(BF16)
        save_ref[chunk] = old_b
        grown = spread_heads(jnp.exp(decay), head_count, head_dim)
        carried = mm_nn(c, old_b) * grown
        last = decay[CHUNK - 1 : CHUNK]
        weight = spread_heads(jnp.exp(last - decay) * step, head_count, head_dim)
        state[...] = old * spread_heads(jnp.exp(last), head_count, head_dim) + mm_tn(
            b, (weight * x).astype(BF16)
        )
        y_ref[pl.ds(start, CHUNK), :] = (within + carried + xt_ref[5:6] * x).astype(BF16)
        return unused

    lax.fori_loop(0, length // CHUNK, chunk_step, 0)


def backward_kernel(
    head_dim,
    proj_ref,
    gy_ref,
    save_ref,
    xt_ref,
    bt_ref,
    heads_ref,
    grad_ref,
    small_x_ref,
    small_b_ref,
    small_h_ref,
    xpad,
    bpad,
    dstate,
    next_x,
    next_b,
):
    length, width = gy_ref.shape
    bc_width = bt_ref.shape[1]
    x_ref, bc_ref, dt_ref = proj_columns(proj_ref, width, bc_width)
    state_size = bc_width // 2
    head_count = width // head_dim
    per_tile = LANES // head_dim
    chunks = length // CHUNK
    xpad[0:PAD] = jnp.zeros((PAD, width), F32)
    bpad[0:PAD] = jnp.zeros((PAD, bc_width), F32)
    xpad[PAD:] = x_ref[...].astype(F32)
    bpad[PAD:] = bc_ref[...].astype(F32)
    dstate[...] = jnp.zeros_like(dstate)
    next_x[...] = jnp.zeros_like(next_x)
    next_b[...] = jnp.zeros_like(next_b)
    small_x_ref[...] = jnp.zeros_like(small_x_ref)
    small_b_ref[...] = jnp.zeros_like(small_b_ref)
    small_h_ref[...] = jnp.zeros_like(small_h_ref)
    row = iota((CHUNK, CHUNK), 0)
    col = iota((CHUNK, CHUNK), 1)
    causal = row >= col
    tril = causal.astype(F32)
    triu = (row <= col).astype(F32)
    strict = (row > col).astype(F32)
    lane = iota((CHUNK, LANES), 1)
    gather_heads = (
        iota((width, LANES), 0) // head_dim == iota((width, LANES), 1)
    ).astype(F32)

    def conv_back(grad_out, pre, padded_rows, taps, following, small_ref):
        gate = sigmoid(pre)
        grad_pre = grad_out * (gate * (1.0 + pre * (1.0 - gate)))
        extended = jnp.concatenate([grad_pre, following[...]], axis=0)
        following[...] = grad_pre[:PAD]
        total = jnp.zeros_like(grad_pre)
        sums = []
        for tap in range(4):
            total = total + taps[tap : tap + 1] * extended[3 - tap : 3 - tap + CHUNK]
            begin = PAD - 3 + tap
            sums.append(
                jnp.sum(grad_pre * padded_rows[begin : begin + CHUNK], axis=0, keepdims=True)
            )
        sums.append(jnp.sum(grad_pre, axis=0, keepdims=True))
        small_ref[0:5] = small_ref[0:5] + jnp.concatenate(sums, axis=0)
        return total

    def chunk_step(index, unused):
        chunk = chunks - 1 - index
        start = pl.multiple_of(chunk * CHUNK, CHUNK)
        x_rows = xpad[pl.ds(start, CHUNK + PAD), :]
        b_rows = bpad[pl.ds(start, CHUNK + PAD), :]
        u_x = conv_pre(x_rows, xt_ref[...])
        x = u_x * sigmoid(u_x)
        u_b = conv_pre(b_rows, bt_ref[...])
        bc = (u_b * sigmoid(u_b)).astype(BF16)
        b, c = bc[:, :state_size], bc[:, state_size:]
        raw, step, decay = decay_terms(
            dt_ref[pl.ds(start, CHUNK), :].astype(F32), heads_ref[...], tril
        )
        rate = heads_ref[1:2]
        decay_t = jnp.transpose(decay)
        step_t = jnp.transpose(step)
        scores = mm_nt(c, b)
        xb = x.astype(BF16)
        gy_b = gy_ref[pl.ds(start, CHUNK), :]
        gy = gy_b.astype(F32)
        old_b = save_ref[chunk]
        dnew = dstate[...]
        dnew_b = dnew.astype(BF16)
        last = decay[CHUNK - 1 : CHUNK]

        dscores = jnp.zeros((CHUNK, CHUNK), F32)
        row_sums = jnp.zeros((CHUNK, LANES), F32)
        col_sums = []
        within = []
        for tile in range(width // LANES):
            lanes = slice(tile * LANES, (tile + 1) * LANES)
            outer = mm_nt(gy_b[:, lanes], split_heads(xb[:, lanes], head_dim))
            mats = []
            for part in range(per_tile):
                head = tile * per_tile + part
                gap = decay[:, head : head + 1] - decay_t[head : head + 1, :]
                fade = jnp.exp(jnp.where(causal, gap, -1e30))
                plain = fade * scores
                mats.append(plain.astype(BF16))
                grad = outer[:, part * CHUNK : (part + 1) * CHUNK]
                scaled = grad * step_t[head : head + 1, :]
                dscores = dscores + scaled * fade
                col_sums.append(jnp.sum(grad * plain, axis=0, keepdims=True))
                rows = jnp.sum(scaled * plain, axis=1, keepdims=True)
                row_sums = row_sums + jnp.where(lane == head, rows, 0.0)
            within.append(
                mm_tn(jnp.concatenate(mats, axis=0), split_heads(gy_b[:, lanes], head_dim))
            )
        within = jnp.concatenate(within, axis=1)
        col_sums.append(jnp.zeros((LANES - head_count, CHUNK), F32))
        col_sums = jnp.transpose(jnp.concatenate(col_sums, axis=0))

        grown_gy = spread_heads(jnp.exp(decay), head_count, head_dim) * gy
        grown_gy_b = grown_gy.astype(BF16)
        remain = jnp.exp(last - decay)
        from_state = spread_heads(remain, head_count, head_dim) * mm_nn(b, dnew_b)
        carried_dot = mm_exact(grown_gy * mm_nn(c, old_b), gather_heads)
        state_dot = mm_exact(x * from_state, gather_heads)
        step_wide = spread_heads(step, head_count, head_dim)
        weight = spread_heads(remain * step, head_count, head_dim)
        dscores_b = dscores.astype(BF16)
        dc = mm_nn(dscores_b, b) + mm_nt(grown_gy_b, old_b)
        db = mm_tn(dscores_b, c) + mm_nt((weight * x).astype(BF16), dnew_b)
        last_wide = spread_heads(jnp.exp(last), head_count, head_dim)
        overlap = jnp.sum(old_b.astype(F32) * dnew, axis=0, keepdims=True) * last_wide
        dlast = mm_exact(jnp.broadcast_to(overlap, (PAD, width)), gather_heads)[0:1]
        dstate[...] = dnew * last_wide + mm_tn(c, grown_gy_b)

        direct = col_sums + state_dot
        ddecay = row_sums + carried_dot - step * col_sums
        da = mm_exact(triu, ddecay) + mm_exact(strict, step * state_dot) + dlast
        dstep = direct + da * rate
        ddt = dstep * sigmoid(raw)
        small_h_ref[0:1] = small_h_ref[0:1] + jnp.sum(ddt, axis=0, keepdims=True)
        small_h_ref[1:2] = small_h_ref[1:2] + jnp.sum(da * step, axis=0, keepdims=True) * rate

        dx = step_wide * (within + from_state) + xt_ref[5:6] * gy
        small_x_ref[5:6] = small_x_ref[5:6] + jnp.sum(gy * x, axis=0, keepdims=True)
        dx_in = conv_back(dx, u_x, x_rows, xt_ref[...], next_x, small_x_ref)
        dbc = jnp.concatenate([db, dc], axis=1)
        dbc_in = conv_back(dbc, u_b, b_rows, bt_ref[...], next_b, small_b_ref)
        grad_ref[pl.ds(start, CHUNK), :] = jnp.concatenate([dx_in, dbc_in, ddt], axis=1).astype(
            BF16
        )
        return unused

    lax.fori_loop(0, chunks, chunk_step, 0)
    small_h_ref[2:3] = mm_exact(
        jnp.broadcast_to(small_x_ref[5:6], (PAD, width)), gather_heads
    )[0:1]


def scan_forward(head_dim, proj, x_taps, bc_taps, heads):
    length = proj.shape[0]
    width, bc_width = x_taps.shape[1], bc_taps.shape[1]
    state_size = bc_width // 2
    chunks = length // CHUNK
    return pl.pallas_call(
        functools.partial(forward_kernel, head_dim),
        out_shape=(
            jax.ShapeDtypeStruct((length, width), BF16),
            jax.ShapeDtypeStruct((chunks, state_size, width), BF16),
        ),
        scratch_shapes=[
            pltpu.VMEM((length + PAD, width), F32),
            pltpu.VMEM((length + PAD, bc_width), F32),
            pltpu.VMEM((state_size, width), F32),
        ],
        compiler_params=pltpu.CompilerParams(vmem_limit_bytes=VMEM_LIMIT),
        cost_estimate=pl.CostEstimate(
            flops=8 * length * width * CHUNK, bytes_accessed=8 * length * width, transcendentals=0
        ),
        name="scan_forward",
    )(proj, x_taps, bc_taps, heads)


def scan_backward(head_dim, proj, gy, saved, x_taps, bc_taps, heads):
    length, width = gy.shape
    bc_width = bc_taps.shape[1]
    state_size = bc_width // 2
    return pl.pallas_call(
        functools.partial(backward_kernel, head_dim),
        out_shape=(
            jax.ShapeDtypeStruct((length, width + bc_width + LANES), BF16),
            jax.ShapeDtypeStruct((PAD, width), F32),
            jax.ShapeDtypeStruct((PAD, bc_width), F32),
            jax.ShapeDtypeStruct((PAD, LANES), F32),
        ),
        scratch_shapes=[
            pltpu.VMEM((length + PAD, width), F32),
            pltpu.VMEM((length + PAD, bc_width), F32),
            pltpu.VMEM((state_size, width), F32),
            pltpu.VMEM((PAD, width), F32),
            pltpu.VMEM((PAD, bc_width), F32),
        ],
        compiler_params=pltpu.CompilerParams(vmem_limit_bytes=VMEM_LIMIT),
        cost_estimate=pl.CostEstimate(
            flops=24 * length * width * CHUNK, bytes_accessed=16 * length * width, transcendentals=0
        ),
        name="scan_backward",
    )(proj, gy, saved, x_taps, bc_taps, heads)


def put(buffer, value, index, axis=0):
    return lax.dynamic_update_index_in_dim(buffer, value, index, axis)


def take(array, index, axis=0):
    return lax.dynamic_index_in_dim(array, index, axis, keepdims=False)


class Ring:
    def __init__(self):
        self.seq = lax.axis_size("seq")
        self.fsdp = lax.axis_size("fsdp")
        self.line = self.fsdp // 2
        self.s = lax.axis_index("seq")
        f = lax.axis_index("fsdp")
        self.p, self.j = f // 2, f % 2

    def from_seq(self, value, k):
        n = self.seq
        return lax.ppermute(value, "seq", [((i + k) % n, i) for i in range(n)])

    def from_line(self, value, k):
        n = self.line
        pairs = [(((i + k) % n) * 2 + c, i * 2 + c) for i in range(n) for c in range(2)]
        return lax.ppermute(value, "fsdp", pairs)

    def from_sibling(self, value):
        return lax.ppermute(value, "fsdp", [(i ^ 1, i) for i in range(self.fsdp)])

    def gather_seq(self, value):
        whole = jnp.zeros((self.seq,) + value.shape, value.dtype)
        for k in range(self.seq):
            part = value if k == 0 else self.from_seq(value, k)
            whole = put(whole, part, (self.s + k) % self.seq)
        return whole

    def gather_line(self, value):
        whole = jnp.zeros((self.line,) + value.shape, value.dtype)
        for k in range(self.line):
            part = value if k == 0 else self.from_line(value, k)
            whole = put(whole, part, (self.p + k) % self.line)
        return whole

    def join_sibling(self, mine):
        other = self.from_sibling(mine)
        whole = jnp.zeros((mine.shape[0], 2) + mine.shape[1:], mine.dtype)
        whole = put(whole, mine, self.j, 1)
        return put(whole, other, 1 - self.j, 1)

    def sum_seq(self, blocks):
        total = take(blocks, self.s).astype(F32)
        for k in range(1, self.seq):
            total = total + self.from_seq(
                take(blocks, (self.s - k) % self.seq), k
            ).astype(F32)
        return total

    def sum_fsdp(self, blocks, extra=None):
        pairs = blocks.reshape((self.line, 2) + blocks.shape[1:])
        mine = take(pairs, self.j, 1).astype(F32)
        other = take(pairs, 1 - self.j, 1).astype(BF16)
        if extra is None:
            mine = mine + self.from_sibling(other).astype(F32)
        else:
            rows = other.shape[0] * other.shape[1]
            sent = jnp.concatenate([other.reshape((rows,) + other.shape[2:]), halves(extra)], axis=0)
            got = self.from_sibling(sent)
            mine = mine + got[:rows].reshape(other.shape).astype(F32)
            extra = extra + whole_of(got[rows:])
        total = take(mine, self.p)
        extra_total = extra
        for k in range(1, self.line):
            sent = take(mine, (self.p - k) % self.line).astype(BF16)
            if extra is None:
                total = total + self.from_line(sent, k).astype(F32)
            else:
                rows = sent.shape[0]
                got = self.from_line(jnp.concatenate([sent, halves(extra)], axis=0), k)
                total = total + got[:rows].astype(F32)
                extra_total = extra_total + whole_of(got[rows:])
        return total, extra_total


def halves(value):
    high = lax.reduce_precision(value, 8, 7)
    return jnp.concatenate([high.astype(BF16), (value - high).astype(BF16)], axis=0)


def whole_of(pair):
    rows = pair.shape[0] // 2
    return pair[:rows].astype(F32) + pair[rows:].astype(F32)


def local(
    tokens,
    norm_gain,
    in_weight,
    dt_weight,
    conv_x_weight,
    conv_x_bias,
    conv_bc_weight,
    conv_bc_bias,
    dt_bias,
    a_log,
    d_skip,
    gate_gain,
    out_weight,
    cotangent,
):
    ring = Ring()
    s, seq, fsdp = ring.s, ring.seq, ring.fsdp
    tok_rows, cot_rows = tokens[0], cotangent[0]
    rows_here, model = tok_rows.shape
    length = rows_here * seq
    inner = gate_gain.shape[0]
    width = inner // seq
    all_heads = dt_bias.shape[0]
    head_dim = inner // all_heads
    heads_here = all_heads // seq
    bc_width = conv_bc_weight.shape[1]
    shard = in_weight.shape[0]
    wide = -(-width // LANES) * LANES

    def columns(array, start, size):
        return lax.dynamic_slice_in_dim(array, start, size, 1)

    def pad_lanes(array, value=0.0, size=LANES):
        return jnp.pad(array, ((0, 0), (0, size - array.shape[1])), constant_values=value)

    x_taps = columns(
        jnp.concatenate(
            [
                conv_x_weight,
                conv_x_bias[None],
                jnp.repeat(d_skip, head_dim)[None],
                gate_gain[None],
                jnp.zeros((1, inner), F32),
            ],
            axis=0,
        ),
        s * width,
        width,
    )
    x_taps = pad_lanes(x_taps, size=wide)
    gain = x_taps[6:7]
    bc_taps = jnp.concatenate(
        [conv_bc_weight, conv_bc_bias[None], jnp.zeros((3, bc_width), F32)], axis=0
    )
    bias_here = columns(dt_bias[None], s * heads_here, heads_here)
    rate_here = -jnp.exp(columns(a_log[None], s * heads_here, heads_here))
    heads = jnp.concatenate(
        [pad_lanes(bias_here, -100.0), pad_lanes(rate_here), jnp.zeros((6, LANES), F32)], axis=0
    )

    own_weight = jnp.concatenate(
        [
            pad_lanes(columns(in_weight, s * width, width), size=wide),
            pad_lanes(columns(in_weight, inner + s * width, width), size=wide),
            in_weight[:, 2 * inner :],
            pad_lanes(columns(dt_weight, s * heads_here, heads_here)),
        ],
        axis=1,
    )
    tok_full = ring.gather_seq(tok_rows).reshape(length, model)
    weight = ring.join_sibling(ring.gather_line(own_weight)).reshape(model, -1)
    cot_full = ring.gather_seq(cot_rows).reshape(length, model)
    out_line = ring.gather_line(out_weight)
    out_rows = ring.line // seq
    out_here = lax.dynamic_slice_in_dim(out_line, s * out_rows, out_rows, 0)
    out_here = ring.join_sibling(out_here).reshape(width, model)
    out_here = jnp.pad(out_here, ((0, wide - width), (0, 0)))

    def rms(rows):
        return lax.rsqrt(jnp.mean(rows * rows, axis=-1, keepdims=True) + EPSILON)

    tok_wide = tok_full.astype(F32)
    scaled = tok_wide * rms(tok_wide)
    normed = (scaled * norm_gain).astype(BF16)
    projected = mm_nn(normed, weight).astype(BF16)
    ssm_out, saved = scan_forward(head_dim, projected, x_taps, bc_taps, heads)
    grad_mixed = mm_nt(cot_full, out_here)
    gate = projected[:, :wide].astype(F32)
    ssm = ssm_out.astype(F32)
    opened = jax.nn.sigmoid(gate)
    silu = gate * opened
    gated = ssm * silu
    gained = grad_mixed * gain
    stats = jnp.stack([jnp.sum(gated * gated, axis=1), jnp.sum(gated * gained, axis=1)])
    stats = stats + sum(ring.from_seq(stats, k) for k in range(1, seq))
    scale = lax.rsqrt(stats[0] / inner + EPSILON)[:, None]
    pull = (scale * scale * scale) * (stats[1][:, None] / inner)
    mixed_plain = gated * scale
    mixed = (mixed_plain * gain).astype(BF16)
    grad_gated = scale * gained - gated * pull
    grad_ssm = (grad_gated * silu).astype(BF16)
    grad_gate = (grad_gated * ssm * (opened * (1.0 + gate * (1.0 - opened)))).astype(BF16)
    gate_gain_part = jnp.sum(grad_mixed * mixed_plain, axis=0)

    out_part = mm_nn(mixed, out_here).astype(BF16).reshape(seq, rows_here, model)
    result = tok_rows.astype(F32) + ring.sum_seq(out_part)

    gate_weight_part = mm_tn(normed, grad_gate)[:, :width].reshape(fsdp, shard, width)
    out_weight_part = mm_tn(mixed, cot_full)[:width].reshape(fsdp, width // fsdp, model)
    early = jnp.concatenate(
        [gate_weight_part]
        + [out_weight_part[:, :, c : c + width] for c in range(0, model, width)],
        axis=1,
    )
    early, unused = ring.sum_fsdp(early)
    total = seq * fsdp
    out_block = lax.ppermute(
        early[shard:].astype(BF16),
        ("seq", "fsdp"),
        [(k, (k % seq) * fsdp + k // seq) for k in range(total)],
    )
    early = ring.gather_seq(jnp.concatenate([early[:shard].astype(BF16), out_block], axis=0))
    gate_weight_grad = early[:, :shard]
    out_weight_grad = early[:, shard:].reshape(seq, model // width, width // fsdp, width)
    out_weight_grad = out_weight_grad.transpose(0, 2, 1, 3).reshape(-1, model).astype(F32)

    grad_cols, small_x, small_bc, small_heads = scan_backward(
        head_dim, projected, grad_ssm, saved, x_taps, bc_taps, heads
    )
    gn_part = mm_nt(grad_gate, weight[:, :wide]) + mm_nt(grad_cols, weight[:, wide:])
    norm_gain_part = jnp.sum(gn_part * scaled, axis=0)
    grad_normed = ring.sum_seq(gn_part.astype(BF16).reshape(seq, rows_here, model))
    late_part = mm_tn(normed, grad_cols).reshape(fsdp, shard, -1)
    late_width = late_part.shape[2]

    pieces = [
        norm_gain_part,
        gate_gain_part[:width],
        small_x[:5, :width].reshape(-1),
        small_bc[:5].reshape(-1),
        small_heads[:3, :heads_here].reshape(-1),
    ]
    sizes = [piece.shape[0] for piece in pieces]
    flat = jnp.concatenate(pieces)
    small_rows = -(-flat.shape[0] // (8 * late_width)) * 8
    flat = jnp.pad(flat, (0, small_rows * late_width - flat.shape[0]))
    late, small = ring.sum_fsdp(late_part, flat.reshape(small_rows, late_width))
    late = ring.gather_seq(jnp.concatenate([late.astype(BF16), halves(small)], axis=0))
    small = (
        late[:, shard : shard + small_rows].astype(F32) + late[:, shard + small_rows :].astype(F32)
    ).reshape(seq, -1)
    parts = []
    at = 0
    for size in sizes:
        parts.append(small[:, at : at + size])
        at += size
    norm_gain_grad = parts[0].sum(0)
    gate_gain_grad = parts[1].reshape(-1)
    conv_x = parts[2].reshape(seq, 5, width).transpose(1, 0, 2).reshape(5, inner)
    conv_bc = parts[3].sum(0).reshape(5, bc_width)
    head_grads = parts[4].reshape(seq, 3, heads_here).transpose(1, 0, 2).reshape(3, all_heads)

    late = late[:, :shard].astype(F32)
    in_weight_grad = jnp.concatenate(
        [
            gate_weight_grad.astype(F32).transpose(1, 0, 2).reshape(shard, inner),
            late[:, :, :width].transpose(1, 0, 2).reshape(shard, inner),
            late[:, :, wide : wide + bc_width].sum(0),
        ],
        axis=1,
    )
    dt_at = wide + bc_width
    dt_weight_grad = late[:, :, dt_at : dt_at + heads_here].transpose(1, 0, 2)
    dt_weight_grad = dt_weight_grad.reshape(shard, all_heads)

    tok_wide = tok_rows.astype(F32)
    scale = rms(tok_wide)
    gained = grad_normed * norm_gain
    grad_tok = scale * gained - tok_wide * (
        scale * scale * scale * jnp.mean(gained * tok_wide, axis=-1, keepdims=True)
    )
    grad_tokens = cot_rows.astype(F32) + grad_tok
    return (
        result[None],
        grad_tokens[None],
        norm_gain_grad,
        in_weight_grad,
        dt_weight_grad,
        conv_x[:4],
        conv_x[4],
        conv_bc[:4],
        conv_bc[4],
        head_grads[0],
        head_grads[1],
        head_grads[2],
        gate_gain_grad,
        out_weight_grad,
    )


def solution(mesh):
    placed = (
        P("fsdp", "seq", None),
        P(),
        P("fsdp", None),
        P("fsdp", None),
        P(),
        P(),
        P(),
        P(),
        P(),
        P(),
        P(),
        P(),
        P("fsdp", None),
        P("fsdp", "seq", None),
    )
    return jax.shard_map(
        local,
        mesh=mesh,
        in_specs=placed,
        out_specs=(
            P("fsdp", "seq", None),
            P("fsdp", "seq", None),
            P(),
            P("fsdp", None),
            P("fsdp", None),
            P(),
            P(),
            P(),
            P(),
            P(),
            P(),
            P(),
            P(),
            P("fsdp", None),
        ),
        check_vma=False,
    )
```

time: 737 us -> 246 us (0.33)
  waiting for transfers between devices: 217 us -> 76.5 us
  local copies, waits for them, and re-layouts: 167 us -> 39.6 us
  matrix products: 119 us -> 22.8 us
  other arithmetic: 106 us -> 15 us
  blocking collectives: 85.7 us -> 0 us
  starting transfers between devices: 19.4 us -> 55.8 us
  Pallas kernels: 0 us -> 33.3 us
  between operations: 15.5 us -> 1.82 us
    reduce_scatter x3 -> x0, waiting for transfers between devices: 150 us -> none  [the longest x1 111 us: local(): lax.psum_scatter(jnp.concatenate([contract_rows(piece, grad_proj), contra...]
    dynamic_update_slice x39 -> x25, local copies, waits for them, and re-layouts: 101 us -> 4.64 us  [put(): return lax.dynamic_update_index_in_dim(buffer, value, index, axis)]
    dot_general x57 -> x8, matrix products: 119 us -> 22.8 us  [mm(): lax.dot_general(left, right, (dims, ((), ())), preferred_element_type=F32)]
    ppermute x0 -> x38, waiting for transfers between devices: none -> 76.5 us  [the longest x12 38.3 us: from_line(): return lax.ppermute(value, 'fsdp', pairs)]
    ppermute x0 -> x38, starting transfers between devices: none -> 55.8 us  [the longest x21 27.9 us: from_seq(): return lax.ppermute(value, 'seq', [((i + k) % n, i) for i in range(n)])]
    another operation x29 -> x2, other arithmetic: 39.4 us -> 0.09 us
    psum x1 -> x0, blocking collectives: 39.1 us -> none  [local(): lax.psum((grad_norm_gain, grad_gate_gain, conv_x_full, conv_xb_full, mixe...]
    pallas_call x0 -> x2, Pallas kernels: none -> 33.3 us  [the longest x1 22.6 us: scan_backward(): pl.pallas_call(functools.partial(backward_kernel, head_dim), out_shape=(j...]
  transfers between devices with their start and end apart: 11 -> 38, of which waited for: 7 -> 15; matrix products, arithmetic and copies ran while one was open for 25% -> 13% of each run, Pallas kernels for 0% -> 0%
where the time goes in v1:
time: 246 us; the launch traced here: 245 us
  waiting for transfers between devices  76.5 us (31%)
  starting transfers between devices  55.8 us (23%)
  local copies, waits for them, and re-layouts  39.6 us (16%)
  Pallas kernels  33.3 us (14%)
  matrix products  22.8 us (9%)
  other arithmetic  15 us (6%)
    ppermute x12, waiting for transfers between devices, from_line(): return lax.ppermute(value, 'fsdp', pairs)  38.3 us
    ppermute x21, waiting for transfers between devices, from_seq(): return lax.ppermute(value, 'seq', [((i + k) % n, i) for i in range(n)])  38.2 us
    ppermute x21, starting transfers between devices, from_seq(): return lax.ppermute(value, 'seq', [((i + k) % n, i) for i in range(n)])  27.9 us
    ppermute x12, starting transfers between devices, from_line(): return lax.ppermute(value, 'fsdp', pairs)  26.1 us
    dot_general x8, matrix products, mm(): lax.dot_general(left, right, (dims, ((), ())), preferred_element_type=F32)  22.8 us
    pallas_call x1, Pallas kernels, scan_backward(): pl.pallas_call(functools.partial(backward_kernel, head_dim), out_shape=(j...  22.6 us
    unnamed x97, local copies, waits for them, and re-layouts  12.6 us
    pallas_call x1, Pallas kernels, scan_forward(): pl.pallas_call(functools.partial(forward_kernel, head_dim), out_shape=(ja...  10.7 us
  transfers between devices with their start and end apart: 38, of which 15 were waited for; matrix products, arithmetic and copies ran while one was open for 13% of the time, Pallas kernels for 0%

profile of v1, /device:TPU:0, one launch (start us, length us, event | category | flops | bytes accessed | tf_op | source)
XLA Modules:
  0.0 244.9 jit_solution(8719376234336750340)
XLA Ops:
  3.9 4.1 %collective-permute-start.4 = (bf16[96,1152]{1,0:T(8,128)(2,1)}, bf16[96,1152]{1,0:T(8,128)(2,1)}, u32[]{:S(2)}, u32[]{:S(2)}) collective-permute-start(bf16[96,1152]{1,0:T(8,128)(2,1)} %fusion.33), channel_id=1, source_target_pairs={{4,0},{5,1},{6,2},{7,3},{0,4},{1,5},{2,6},{3,7},{12,8},{13,9},{14,... | collective-permute-start | bytes 663560 | tf_op jit(solution)/shard_map/ppermute | solution.py:396
  10.0 3.1 %collective-permute-start.10 = (bf16[192,768]{1,0:T(8,128)(2,1)}, bf16[192,768]{1,0:T(8,128)(2,1)}, u32[]{:S(2)}, u32[]{:S(2)}) collective-permute-start(bf16[192,768]{1,0:T(8,128)(2,1)} %param.26), channel_id=1, source_target_pairs={{2,0},{3,1},{4,2},{5,3},{6,4},{7,5},{0,6},{1,7},{10,8},{11,9},{12,... | collective-permute-start | bytes 884744 | tf_op jit(solution)/shard_map/ppermute | solution.py:396
  21.5 2.9 %collective-permute-done.3 = bf16[96,1152]{1,0:T(8,128)(2,1)} collective-permute-done((bf16[96,1152]{1,0:T(8,128)(2,1)}, bf16[96,1152]{1,0:T(8,128)(2,1)}, u32[]{:S(2)}, u32[]{:S(2)}) %collective-permute-start.3) | collective-permute-done | bytes 221216 | tf_op jit(solution)/shard_map/ppermute | solution.py:396
  24.4 4.0 %collective-permute-start.11 = (bf16[192,768]{1,0:T(8,128)(2,1)S(1)}, bf16[192,768]{1,0:T(8,128)(2,1)S(1)}, u32[]{:S(2)}, u32[]{:S(2)}) collective-permute-start(bf16[192,768]{1,0:T(8,128)(2,1)S(1)} %copy-done.27), channel_id=1, source_target_pairs={{4,0},{5,1},{6,2},{7,3},{0,4},{1,5},{2,6},{3,7},{12,8},{13,9},{14,... | collective-permute-start | bytes 884744 | tf_op jit(solution)/shard_map/ppermute | solution.py:396
  37.5 15.7 %collective-permute-done.11 = bf16[192,768]{1,0:T(8,128)(2,1)S(1)} collective-permute-done((bf16[192,768]{1,0:T(8,128)(2,1)S(1)}, bf16[192,768]{1,0:T(8,128)(2,1)S(1)}, u32[]{:S(2)}, u32[]{:S(2)}) %collective-permute-start.11) | collective-permute-done | bytes 294944 | tf_op jit(solution)/shard_map/ppermute | solution.py:396
  53.2 2.5 %collective-permute-start = (bf16[256,768]{1,0:T(8,128)(2,1)S(1)}, bf16[256,768]{1,0:T(8,128)(2,1)S(1)}, u32[]{:S(2)}, u32[]{:S(2)}) collective-permute-start(bf16[256,768]{1,0:T(8,128)(2,1)S(1)} %bitcast.213), channel_id=1, source_target_pairs={{8,0},{16,8},{24,16},{0,24},{9,1},{17,9},{25,17},{1,25},{10,2},{18... | collective-permute-start | bytes 1179656 | tf_op jit(solution)/shard_map/ppermute | solution.py:391
  56.4 7.0 %collective-permute-done = bf16[256,768]{1,0:T(8,128)(2,1)S(1)} collective-permute-done((bf16[256,768]{1,0:T(8,128)(2,1)S(1)}, bf16[256,768]{1,0:T(8,128)(2,1)S(1)}, u32[]{:S(2)}, u32[]{:S(2)}) %collective-permute-start) | collective-permute-done | bytes 393248 | tf_op jit(solution)/shard_map/ppermute | solution.py:391
  63.5 2.3 collective-permute-start.2
  66.6 7.5 %collective-permute-done.2 = bf16[256,768]{1,0:T(8,128)(2,1)S(1)} collective-permute-done((bf16[256,768]{1,0:T(8,128)(2,1)S(1)}, bf16[256,768]{1,0:T(8,128)(2,1)S(1)}, u32[]{:S(2)}, u32[]{:S(2)}) %collective-permute-start.2) | collective-permute-done | bytes 393248 | tf_op jit(solution)/shard_map/ppermute | solution.py:391
  78.3 3.6 %convolution_convert_fusion.proj_ref = bf16[1024,1152]{1,0:T(8,128)(2,1)} fusion(bf16[1024,768]{1,0:T(8,128)(2,1)S(1)} %bitcast.226, bf16[768,1152]{1,0:T(8,128)(2,1)S(1)} %bitcast.216), kind=kOutput, calls=%fused_computation | convolution fusion | flops 1813118976 | bytes 5701632 | tf_op jit(solution)/shard_map/dot_general | solution.py:20
  82.0 10.7 %scan_forward.1 = (bf16[1024,384]{1,0:T(8,128)(2,1)}, bf16[8,128,384]{2,1,0:T(8,128)(2,1)}) custom-call(bf16[1024,1152]{1,0:T(8,128)(2,1)} %convolution_convert_fusion.proj_ref, f32[8,384]{1,0:T(8,128)} %constant_dynamic-slice_fusion.1.xt_ref, f32[8,256]{1,0:T(8,128)} %maximum_maximum_fusion.bt_ref, f32[8,128]{1,0:T(8,128)} %fusion.46.heads_ref), custom_call_target="tpu_custom_call" | custom-call | flops 402653184 | bytes 3145728 | tf_op jit(solution)/shard_map/scan_forward/pallas_call | solution.py:326
  92.7 4.1 %multiply_reduce_fusion.4 = (f32[1024]{0:T(1024)S(1)}, f32[1024]{0:T(1024)S(1)}, f32[1024,384]{1,0:T(8,128)}) fusion(bf16[1024,1152]{1,0:T(8,128)(2,1)} %convolution_convert_fusion.proj_ref, bf16[1024,384]{1,0:T(8,128)(2,1)} %get-tuple-element.20, f32[384]{0:T(512)S(1)} %copy-done.34, bf16[1024,768]{1,0:T(8,128)(2,1)S(1)} %bitcast.230, ...), kind=kOutput, calls=%fused_computation.28 | convolution fusion | flops 608696320 | bytes 5318144 | tf_op jit(solution)/shard_map/dot_general | solution.py:20
  102.9 4.2 %convolution_convert_fusion.1 = bf16[1024,768]{1,0:T(8,128)(2,1)} fusion(bf16[384,768]{1,0:T(8,128)(2,1)} %bitcast.238, f32[1024]{0:T(1024)S(1)} %bitcast.246, f32[384]{0:T(512)} %dynamic-slice_reduce_fusion, bf16[1024,384]{1,0:T(8,128)(2,1)} %get-tuple-element.20, bf16[1024,1152]{1,0:T(8,128)(2,1)} %convolution_convert_fusion.proj_ref), kind=kOutput, calls=%fused_computation.13 | convolution fusion | flops 608698368 | bytes 3741696 | tf_op jit(solution)/shard_map/dot_general | solution.py:20
  107.1 4.1 %fusion.1 = (bf16[1024,384]{1,0:T(8,128)(2,1)}, bf16[1024,384]{1,0:T(8,128)(2,1)}, f32[384]{0:T(512)}, bf16[384,1024]{0,1:T(8,128)(2,1)S(1)}) fusion(bf16[1024,384]{1,0:T(8,128)(2,1)S(1)} %copy-done.22, f32[1024]{0:T(1024)S(1)} %fusion.43, f32[1024,384]{1,0:T(8,128)S(1)} %copy-done.19, f32[384]{0:T(512)S(1)} %copy-done.35, f32[1024]{0:T(1024)S(1)} %bitcast.248, ...), kind=kLoop, calls=%fused_computation.15 | loop fusion | flops 9830016 | bytes 5516288 | tf_op jit(solution)/shard_map/convert_element_type | solution.py:567
  111.3 22.6 %scan_backward.1 = (bf16[1024,768]{1,0:T(8,128)(2,1)}, f32[8,384]{1,0:T(8,128)}, f32[8,256]{1,0:T(8,128)}, f32[8,128]{1,0:T(8,128)}) custom-call(bf16[1024,1152]{1,0:T(8,128)(2,1)} %convolution_convert_fusion.proj_ref, bf16[1024,384]{1,0:T(8,128)(2,1)} %get-tuple-element.38.gy_ref, bf16[8,128,384]{2,1,0:T(8,128)(2,1)} %get-tuple-element.21.save_ref, ...), custom_call_target="tpu_custom_call" | custom-call | flops 1207959552 | bytes 6291456 | tf_op jit(solution)/shard_map/scan_backward/pallas_call | solution.py:349
  137.5 2.3 fusion.54
  142.7 2.2 collective-permute-start.17
  146.4 3.1 %multiply_reduce_fusion = (f32[768]{0:T(1024)}, bf16[1024,768]{1,0:T(8,128)(2,1)S(1)}, bf16[1024,768]{1,0:T(8,128)(2,1)}) fusion(bf16[4,256,768]{2,1,0:T(8,128)(2,1)S(1)} %bitcast_dynamic-update-slice_fusion.5, f32[1024]{0:T(1024)S(1)} %bitcast.251, f32[768]{0:T(1024)S(1)} %copy-done.28, f32[1024,768]{1,0:T(8,128)S(1)} %fusion.9, ...), kind=kOutput, calls=%fused_computation.2 | convolution fusion | flops 610270464 | bytes 9251840 | tf_op jit(solution)/shard_map/dot_general | solution.py:20
  150.5 2.9 %collective-permute-start.20 = (bf16[256,768]{1,0:T(8,128)(2,1)}, bf16[256,768]{1,0:T(8,128)(2,1)}, u32[]{:S(2)}, u32[]{:S(2)}) collective-permute-start(bf16[256,768]{1,0:T(8,128)(2,1)} %get-tuple-element.44), channel_id=1, source_target_pairs={{8,0},{16,8},{24,16},{0,24},{9,1},{17,9},{25,17},{1,25},{10,2},{18... | collective-permute-start | bytes 1179656 | tf_op jit(solution)/shard_map/ppermute | solution.py:391
  156.4 2.7 %fusion.22 = f32[8,96,384]{2,1,0:T(8,128)S(1)} fusion(bf16[8,96,1024]{2,1,0:T(8,128)(2,1)} %bitcast.227, bf16[1024,384]{1,0:T(8,128)(2,1)} %get-tuple-element.37), kind=kOutput, calls=%fused_computation.55 | convolution fusion | flops 603979776 | bytes 3538944 | tf_op jit(solution)/shard_map/dot_general | solution.py:20
  165.7 6.2 %collective-permute-done.20 = bf16[256,768]{1,0:T(8,128)(2,1)} collective-permute-done((bf16[256,768]{1,0:T(8,128)(2,1)}, bf16[256,768]{1,0:T(8,128)(2,1)}, u32[]{:S(2)}, u32[]{:S(2)}) %collective-permute-start.20) | collective-permute-done | bytes 393248 | tf_op jit(solution)/shard_map/ppermute | solution.py:391
  172.9 4.3 %collective-permute-done.22 = bf16[256,768]{1,0:T(8,128)(2,1)} collective-permute-done((bf16[256,768]{1,0:T(8,128)(2,1)}, bf16[256,768]{1,0:T(8,128)(2,1)}, u32[]{:S(2)}, u32[]{:S(2)}) %collective-permute-start.22) | collective-permute-done | bytes 393248 | tf_op jit(solution)/shard_map/ppermute | solution.py:391
  179.4 4.5 %collective-permute-done.18 = bf16[256,768]{1,0:T(8,128)(2,1)S(1)} collective-permute-done((bf16[256,768]{1,0:T(8,128)(2,1)}, bf16[256,768]{1,0:T(8,128)(2,1)S(1)}, u32[]{:S(2)}, u32[]{:S(2)}) %collective-permute-start.18) | collective-permute-done | bytes 393248 | tf_op jit(solution)/shard_map/ppermute | solution.py:391
  183.8 3.5 %fusion.16 = (f32[1,256,768]{2,1,0:T(8,128)}, f32[1,256,768]{2,1,0:T(8,128)}) fusion(f32[256]{0:T(256)S(1)} %get-tuple-element.78, f32[256]{0:T(256)S(1)} %get-tuple-element.77, f32[768]{0:T(1024)S(1)} %copy-done.28, bf16[256,768]{1,0:T(8,128)(2,1)} %collective-permute-done.22, bf16[256,768]{1,0:T(8,128)(2,1)} %collective-permute-done.21, ...), kind=kLoop, calls=%fused_computation.47 | loop fusion | flops 4325376 | bytes 5510148 | tf_op jit(solution)/shard_map/broadcast_in_dim | solution.py:650
  187.5 4.9 %collective-permute-start.31 = (bf16[192,384]{1,0:T(8,128)(2,1)S(1)}, bf16[192,384]{1,0:T(8,128)(2,1)S(1)}, u32[]{:S(2)}, u32[]{:S(2)}) collective-permute-start(bf16[192,384]{1,0:T(8,128)(2,1)S(1)} %get-tuple-element.50), channel_id=1, source_target_pairs={{2,0},{3,1},{4,2},{5,3},{6,4},{7,5},{0,6},{1,7},{10,8},{11,9},{12,... | collective-permute-start | bytes 442376 | tf_op jit(solution)/shard_map/ppermute | solution.py:396
  194.0 3.2 %collective-permute-start.24 = (bf16[112,768]{1,0:T(8,128)(2,1)S(1)}, bf16[112,768]{1,0:T(8,128)(2,1)S(1)}, u32[]{:S(2)}, u32[]{:S(2)}) collective-permute-start(bf16[112,768]{1,0:T(8,128)(2,1)S(1)} %get-tuple-element.68), channel_id=1, source_target_pairs={{2,0},{3,1},{4,2},{5,3},{6,4},{7,5},{0,6},{1,7},{10,8},{11,9},{12,... | collective-permute-start | bytes 516104 | tf_op jit(solution)/shard_map/ppermute | solution.py:396
  197.2 2.0 collective-permute-start.25
  201.2 6.4 %collective-permute-done.32 = bf16[192,384]{1,0:T(8,128)(2,1)S(1)} collective-permute-done((bf16[192,384]{1,0:T(8,128)(2,1)S(1)}, bf16[192,384]{1,0:T(8,128)(2,1)S(1)}, u32[]{:S(2)}, u32[]{:S(2)}) %collective-permute-start.32) | collective-permute-done | bytes 147488 | tf_op jit(solution)/shard_map/ppermute | solution.py:396
  208.5 13.3 %collective-permute-done.25 = bf16[112,768]{1,0:T(8,128)(2,1)S(1)} collective-permute-done((bf16[112,768]{1,0:T(8,128)(2,1)S(1)}, bf16[112,768]{1,0:T(8,128)(2,1)S(1)}, u32[]{:S(2)}, u32[]{:S(2)}) %collective-permute-start.25) | collective-permute-done | bytes 172064 | tf_op jit(solution)/shard_map/ppermute | solution.py:396
  224.2 2.0 collective-permute-start.36
  227.2 2.1 collective-permute-done.27
  230.8 3.6 %collective-permute-done.29 = bf16[112,768]{1,0:T(8,128)(2,1)S(1)} collective-permute-done((bf16[112,768]{1,0:T(8,128)(2,1)S(1)}, bf16[112,768]{1,0:T(8,128)(2,1)S(1)}, u32[]{:S(2)}, u32[]{:S(2)}) %collective-permute-start.29) | collective-permute-done | bytes 172064 | tf_op jit(solution)/shard_map/ppermute | solution.py:391
  (280 shorter events, 75.3 us)
Async XLA Ops:
  3.9 25.4 %collective-permute-start.4 = (bf16[96,1152]{1,0:T(8,128)(2,1)}, bf16[96,1152]{1,0:T(8,128)(2,1)}, u32[]{:S(2)}, u32[]{:S(2)}) collective-permute-start(bf16[96,1152]{1,0:T(8,128)(2,1)} %fusion.33), channel_id=1, source_target_pairs={{4,0},{5,1},{6,2},{7,3},{0,4},{1,5},{2,6},{3,7},{12,8},{13,9},{14,... | collective-permute-start | bytes 663560 | tf_op jit(solution)/shard_map/ppermute | solution.py:396
  8.0 16.4 %collective-permute-start.3 = (bf16[96,1152]{1,0:T(8,128)(2,1)}, bf16[96,1152]{1,0:T(8,128)(2,1)}, u32[]{:S(2)}, u32[]{:S(2)}) collective-permute-start(bf16[96,1152]{1,0:T(8,128)(2,1)} %fusion.33), channel_id=1, source_target_pairs={{2,0},{3,1},{4,2},{5,3},{6,4},{7,5},{0,6},{1,7},{10,8},{11,9},{12,... | collective-permute-start | bytes 663560 | tf_op jit(solution)/shard_map/ppermute | solution.py:396
  9.3 22.8 %collective-permute-start.5 = (bf16[96,1152]{1,0:T(8,128)(2,1)}, bf16[96,1152]{1,0:T(8,128)(2,1)}, u32[]{:S(2)}, u32[]{:S(2)}) collective-permute-start(bf16[96,1152]{1,0:T(8,128)(2,1)} %fusion.33), channel_id=1, source_target_pairs={{6,0},{7,1},{0,2},{1,3},{2,4},{3,5},{4,6},{5,7},{14,8},{15,9},{8,1... | collective-permute-start | bytes 663560 | tf_op jit(solution)/shard_map/ppermute | solution.py:396
  10.0 25.0 %collective-permute-start.10 = (bf16[192,768]{1,0:T(8,128)(2,1)}, bf16[192,768]{1,0:T(8,128)(2,1)}, u32[]{:S(2)}, u32[]{:S(2)}) collective-permute-start(bf16[192,768]{1,0:T(8,128)(2,1)} %param.26), channel_id=1, source_target_pairs={{2,0},{3,1},{4,2},{5,3},{6,4},{7,5},{0,6},{1,7},{10,8},{11,9},{12,... | collective-permute-start | bytes 884744 | tf_op jit(solution)/shard_map/ppermute | solution.py:396
  13.2 42.5 %collective-permute-start.12 = (bf16[192,768]{1,0:T(8,128)(2,1)}, bf16[192,768]{1,0:T(8,128)(2,1)S(1)}, u32[]{:S(2)}, u32[]{:S(2)}) collective-permute-start(bf16[192,768]{1,0:T(8,128)(2,1)} %param.26), channel_id=1, source_target_pairs={{6,0},{7,1},{0,2},{1,3},{2,4},{3,5},{4,6},{5,7},{14,8},{15,9},{8,1... | collective-permute-start | bytes 884744 | tf_op jit(solution)/shard_map/ppermute | solution.py:396
  24.4 28.8 %collective-permute-start.11 = (bf16[192,768]{1,0:T(8,128)(2,1)S(1)}, bf16[192,768]{1,0:T(8,128)(2,1)S(1)}, u32[]{:S(2)}, u32[]{:S(2)}) collective-permute-start(bf16[192,768]{1,0:T(8,128)(2,1)S(1)} %copy-done.27), channel_id=1, source_target_pairs={{4,0},{5,1},{6,2},{7,3},{0,4},{1,5},{2,6},{3,7},{12,8},{13,9},{14,... | collective-permute-start | bytes 884744 | tf_op jit(solution)/shard_map/ppermute | solution.py:396
  29.4 45.2 %collective-permute-start.9 = (bf16[256,768]{1,0:T(8,128)(2,1)S(1)}, bf16[256,768]{1,0:T(8,128)(2,1)S(1)}, u32[]{:S(2)}, u32[]{:S(2)}) collective-permute-start(bf16[256,768]{1,0:T(8,128)(2,1)S(1)} %bitcast.231), channel_id=1, source_target_pairs={{24,0},{0,8},{8,16},{16,24},{25,1},{1,9},{9,17},{17,25},{26,2},{2,... | collective-permute-start | bytes 1179656 | tf_op jit(solution)/shard_map/ppermute | solution.py:391
  32.2 34.3 %collective-permute-start.8 = (bf16[256,768]{1,0:T(8,128)(2,1)S(1)}, bf16[256,768]{1,0:T(8,128)(2,1)S(1)}, u32[]{:S(2)}, u32[]{:S(2)}) collective-permute-start(bf16[256,768]{1,0:T(8,128)(2,1)S(1)} %bitcast.232), channel_id=1, source_target_pairs={{16,0},{24,8},{0,16},{8,24},{17,1},{25,9},{1,17},{9,25},{18,2},{26... | collective-permute-start | bytes 1179656 | tf_op jit(solution)/shard_map/ppermute | solution.py:391
  35.0 30.7 %collective-permute-start.7 = (bf16[256,768]{1,0:T(8,128)(2,1)S(1)}, bf16[256,768]{1,0:T(8,128)(2,1)S(1)}, u32[]{:S(2)}, u32[]{:S(2)}) collective-permute-start(bf16[256,768]{1,0:T(8,128)(2,1)S(1)} %bitcast.233), channel_id=1, source_target_pairs={{8,0},{16,8},{24,16},{0,24},{9,1},{17,9},{25,17},{1,25},{10,2},{18... | collective-permute-start | bytes 1179656 | tf_op jit(solution)/shard_map/ppermute | solution.py:391
  53.2 10.3 %collective-permute-start = (bf16[256,768]{1,0:T(8,128)(2,1)S(1)}, bf16[256,768]{1,0:T(8,128)(2,1)S(1)}, u32[]{:S(2)}, u32[]{:S(2)}) collective-permute-start(bf16[256,768]{1,0:T(8,128)(2,1)S(1)} %bitcast.213), channel_id=1, source_target_pairs={{8,0},{16,8},{24,16},{0,24},{9,1},{17,9},{25,17},{1,25},{10,2},{18... | collective-permute-start | bytes 1179656 | tf_op jit(solution)/shard_map/ppermute | solution.py:391
  55.7 10.2 %collective-permute-start.1 = (bf16[256,768]{1,0:T(8,128)(2,1)S(1)}, bf16[256,768]{1,0:T(8,128)(2,1)S(1)}, u32[]{:S(2)}, u32[]{:S(2)}) collective-permute-start(bf16[256,768]{1,0:T(8,128)(2,1)S(1)} %bitcast.214), channel_id=1, source_target_pairs={{16,0},{24,8},{0,16},{8,24},{17,1},{25,9},{1,17},{9,25},{18,2},{26... | collective-permute-start | bytes 1179656 | tf_op jit(solution)/shard_map/ppermute | solution.py:391
  63.5 10.6 %collective-permute-start.2 = (bf16[256,768]{1,0:T(8,128)(2,1)S(1)}, bf16[256,768]{1,0:T(8,128)(2,1)S(1)}, u32[]{:S(2)}, u32[]{:S(2)}) collective-permute-start(bf16[256,768]{1,0:T(8,128)(2,1)S(1)} %bitcast.215), channel_id=1, source_target_pairs={{24,0},{0,8},{8,16},{16,24},{25,1},{1,9},{9,17},{17,25},{26,2},{2,... | collective-permute-start | bytes 1179656 | tf_op jit(solution)/shard_map/ppermute | solution.py:391
  65.8 10.5 %collective-permute-start.6 = (bf16[4,96,1152]{2,1,0:T(8,128)(2,1)S(1)}, bf16[4,96,1152]{2,1,0:T(8,128)(2,1)S(1)}, u32[]{:S(2)}, u32[]{:S(2)}) collective-permute-start(bf16[4,96,1152]{2,1,0:T(8,128)(2,1)S(1)} %bitcast_dynamic-update-slice_fusion.14), channel_id=1, source_target_pairs={{1,0},{0,1},{3,2},{2,3},{5,4},{4,5},{7,6},{6,7},{9,8},{8,9},{11,10... | collective-permute-start | bytes 2654216 | tf_op jit(solution)/shard_map/ppermute | solution.py:399
  65.9 10.3 %collective-permute-start.13 = (bf16[1,192,768]{2,1,0:T(8,128)(2,1)S(1)}, bf16[1,192,768]{2,1,0:T(8,128)(2,1)S(1)}, u32[]{:S(2)}, u32[]{:S(2)}) collective-permute-start(bf16[1,192,768]{2,1,0:T(8,128)(2,1)S(1)} %get-tuple-element.36), channel_id=1, source_target_pairs={{1,0},{0,1},{3,2},{2,3},{5,4},{4,5},{7,6},{6,7},{9,8},{8,9},{11,10... | collective-permute-start | bytes 884744 | tf_op jit(solution)/shard_map/ppermute | solution.py:399
  142.7 36.6 %collective-permute-start.17 = (bf16[256,768]{1,0:T(8,128)(2,1)}, bf16[256,768]{1,0:T(8,128)(2,1)}, u32[]{:S(2)}, u32[]{:S(2)}) collective-permute-start(bf16[256,768]{1,0:T(8,128)(2,1)} %get-tuple-element.47), channel_id=1, source_target_pairs={{8,0},{16,8},{24,16},{0,24},{9,1},{17,9},{25,17},{1,25},{10,2},{18... | collective-permute-start | bytes 1179656 | tf_op jit(solution)/shard_map/ppermute | solution.py:391
  144.9 34.4 %collective-permute-start.19 = (bf16[256,768]{1,0:T(8,128)(2,1)}, bf16[256,768]{1,0:T(8,128)(2,1)}, u32[]{:S(2)}, u32[]{:S(2)}) collective-permute-start(bf16[256,768]{1,0:T(8,128)(2,1)} %get-tuple-element.48), channel_id=1, source_target_pairs={{24,0},{0,8},{8,16},{16,24},{25,1},{1,9},{9,17},{17,25},{26,2},{2,... | collective-permute-start | bytes 1179656 | tf_op jit(solution)/shard_map/ppermute | solution.py:391
  150.5 21.4 %collective-permute-start.20 = (bf16[256,768]{1,0:T(8,128)(2,1)}, bf16[256,768]{1,0:T(8,128)(2,1)}, u32[]{:S(2)}, u32[]{:S(2)}) collective-permute-start(bf16[256,768]{1,0:T(8,128)(2,1)} %get-tuple-element.44), channel_id=1, source_target_pairs={{8,0},{16,8},{24,16},{0,24},{9,1},{17,9},{25,17},{1,25},{10,2},{18... | collective-permute-start | bytes 1179656 | tf_op jit(solution)/shard_map/ppermute | solution.py:391
  153.5 23.7 %collective-permute-start.22 = (bf16[256,768]{1,0:T(8,128)(2,1)}, bf16[256,768]{1,0:T(8,128)(2,1)}, u32[]{:S(2)}, u32[]{:S(2)}) collective-permute-start(bf16[256,768]{1,0:T(8,128)(2,1)} %get-tuple-element.45), channel_id=1, source_target_pairs={{24,0},{0,8},{8,16},{16,24},{25,1},{1,9},{9,17},{17,25},{26,2},{2,... | collective-permute-start | bytes 1179656 | tf_op jit(solution)/shard_map/ppermute | solution.py:391
  153.5 23.7 %collective-permute-start.21 = (bf16[256,768]{1,0:T(8,128)(2,1)}, bf16[256,768]{1,0:T(8,128)(2,1)}, u32[]{:S(2)}, u32[]{:S(2)}) collective-permute-start(bf16[256,768]{1,0:T(8,128)(2,1)} %get-tuple-element.46), channel_id=1, source_target_pairs={{16,0},{24,8},{0,16},{8,24},{17,1},{25,9},{1,17},{9,25},{18,2},{26... | collective-permute-start | bytes 1179656 | tf_op jit(solution)/shard_map/ppermute | solution.py:391
  172.0 11.9 %collective-permute-start.18 = (bf16[256,768]{1,0:T(8,128)(2,1)}, bf16[256,768]{1,0:T(8,128)(2,1)S(1)}, u32[]{:S(2)}, u32[]{:S(2)}) collective-permute-start(bf16[256,768]{1,0:T(8,128)(2,1)} %get-tuple-element.49), channel_id=1, source_target_pairs={{16,0},{24,8},{0,16},{8,24},{17,1},{25,9},{1,17},{9,25},{18,2},{26... | collective-permute-start | bytes 1179656 | tf_op jit(solution)/shard_map/ppermute | solution.py:391
  177.2 10.2 %collective-permute-start.30 = (bf16[4,192,384]{2,1,0:T(8,128)(2,1)S(1)}, bf16[4,192,384]{2,1,0:T(8,128)(2,1)S(1)}, u32[]{:S(2)}, u32[]{:S(2)}) collective-permute-start(bf16[4,192,384]{2,1,0:T(8,128)(2,1)S(1)} %copy-done.23), channel_id=1, source_target_pairs={{1,0},{0,1},{3,2},{2,3},{5,4},{4,5},{7,6},{6,7},{9,8},{8,9},{11,10... | collective-permute-start | bytes 1769480 | tf_op jit(solution)/shard_map/ppermute | solution.py:399
  177.2 15.9 %collective-permute-start.23 = (bf16[400,768]{1,0:T(8,128)(2,1)S(1)}, bf16[400,768]{1,0:T(8,128)(2,1)S(1)}, u32[]{:S(2)}, u32[]{:S(2)}) collective-permute-start(bf16[400,768]{1,0:T(8,128)(2,1)S(1)} %pad_maximum_fusion.2), channel_id=1, source_target_pairs={{1,0},{0,1},{3,2},{2,3},{5,4},{4,5},{7,6},{6,7},{9,8},{8,9},{11,10... | collective-permute-start | bytes 1843208 | tf_op jit(solution)/shard_map/ppermute | solution.py:399
  187.5 11.7 %collective-permute-start.31 = (bf16[192,384]{1,0:T(8,128)(2,1)S(1)}, bf16[192,384]{1,0:T(8,128)(2,1)S(1)}, u32[]{:S(2)}, u32[]{:S(2)}) collective-permute-start(bf16[192,384]{1,0:T(8,128)(2,1)S(1)} %get-tuple-element.50), channel_id=1, source_target_pairs={{2,0},{3,1},{4,2},{5,3},{6,4},{7,5},{0,6},{1,7},{10,8},{11,9},{12,... | collective-permute-start | bytes 442376 | tf_op jit(solution)/shard_map/ppermute | solution.py:396
  192.4 15.2 %collective-permute-start.32 = (bf16[192,384]{1,0:T(8,128)(2,1)S(1)}, bf16[192,384]{1,0:T(8,128)(2,1)S(1)}, u32[]{:S(2)}, u32[]{:S(2)}) collective-permute-start(bf16[192,384]{1,0:T(8,128)(2,1)S(1)} %get-tuple-element.52), channel_id=1, source_target_pairs={{4,0},{5,1},{6,2},{7,3},{0,4},{1,5},{2,6},{3,7},{12,8},{13,9},{14,... | collective-permute-start | bytes 442376 | tf_op jit(solution)/shard_map/ppermute | solution.py:396
  194.0 14.5 %collective-permute-start.24 = (bf16[112,768]{1,0:T(8,128)(2,1)S(1)}, bf16[112,768]{1,0:T(8,128)(2,1)S(1)}, u32[]{:S(2)}, u32[]{:S(2)}) collective-permute-start(bf16[112,768]{1,0:T(8,128)(2,1)S(1)} %get-tuple-element.68), channel_id=1, source_target_pairs={{2,0},{3,1},{4,2},{5,3},{6,4},{7,5},{0,6},{1,7},{10,8},{11,9},{12,... | collective-permute-start | bytes 516104 | tf_op jit(solution)/shard_map/ppermute | solution.py:396
  197.2 24.5 %collective-permute-start.25 = (bf16[112,768]{1,0:T(8,128)(2,1)S(1)}, bf16[112,768]{1,0:T(8,128)(2,1)S(1)}, u32[]{:S(2)}, u32[]{:S(2)}) collective-permute-start(bf16[112,768]{1,0:T(8,128)(2,1)S(1)} %get-tuple-element.69), channel_id=1, source_target_pairs={{4,0},{5,1},{6,2},{7,3},{0,4},{1,5},{2,6},{3,7},{12,8},{13,9},{14,... | collective-permute-start | bytes 516104 | tf_op jit(solution)/shard_map/ppermute | solution.py:396
  199.3 22.5 %collective-permute-start.26 = (bf16[112,768]{1,0:T(8,128)(2,1)S(1)}, bf16[112,768]{1,0:T(8,128)(2,1)S(1)}, u32[]{:S(2)}, u32[]{:S(2)}) collective-permute-start(bf16[112,768]{1,0:T(8,128)(2,1)S(1)} %get-tuple-element.70), channel_id=1, source_target_pairs={{6,0},{7,1},{0,2},{1,3},{2,4},{3,5},{4,6},{5,7},{14,8},{15,9},{8,1... | collective-permute-start | bytes 516104 | tf_op jit(solution)/shard_map/ppermute | solution.py:396
  207.8 16.3 %collective-permute-start.34 = (bf16[96,384]{1,0:T(8,128)(2,1)S(1)}, bf16[96,384]{1,0:T(8,128)(2,1)S(1)}, u32[]{:S(2)}, u32[]{:S(2)}) collective-permute-start(bf16[96,384]{1,0:T(8,128)(2,1)S(1)} %get-tuple-element.67), channel_id=1, source_target_pairs={{0,0},{1,8},{2,16},{3,24},{4,1},{5,9},{6,17},{7,25},{8,2},{9,10},{... | collective-permute-start | bytes 221192 | tf_op jit(solution)/shard_map/ppermute | solution.py:582
  221.9 8.9 %collective-permute-start.28 = (bf16[112,768]{1,0:T(8,128)(2,1)S(1)}, bf16[112,768]{1,0:T(8,128)(2,1)S(1)}, u32[]{:S(2)}, u32[]{:S(2)}) collective-permute-start(bf16[112,768]{1,0:T(8,128)(2,1)S(1)} %pad_maximum_fusion.9), channel_id=1, source_target_pairs={{16,0},{24,8},{0,16},{8,24},{17,1},{25,9},{1,17},{9,25},{18,2},{26... | collective-permute-start | bytes 516104 | tf_op jit(solution)/shard_map/ppermute | solution.py:391
  222.8 11.7 %collective-permute-start.29 = (bf16[112,768]{1,0:T(8,128)(2,1)S(1)}, bf16[112,768]{1,0:T(8,128)(2,1)S(1)}, u32[]{:S(2)}, u32[]{:S(2)}) collective-permute-start(bf16[112,768]{1,0:T(8,128)(2,1)S(1)} %pad_maximum_fusion.9), channel_id=1, source_target_pairs={{24,0},{0,8},{8,16},{16,24},{25,1},{1,9},{9,17},{17,25},{26,2},{2,... | collective-permute-start | bytes 516104 | tf_op jit(solution)/shard_map/ppermute | solution.py:391
  224.2 11.1 %collective-permute-start.36 = (bf16[192,384]{1,0:T(8,128)(2,1)S(1)}, bf16[192,384]{1,0:T(8,128)(2,1)S(1)}, u32[]{:S(2)}, u32[]{:S(2)}) collective-permute-start(bf16[192,384]{1,0:T(8,128)(2,1)S(1)} %pad_maximum_fusion.10), channel_id=1, source_target_pairs={{16,0},{24,8},{0,16},{8,24},{17,1},{25,9},{1,17},{9,25},{18,2},{26... | collective-permute-start | bytes 442376 | tf_op jit(solution)/shard_map/ppermute | solution.py:391
  226.2 9.0 %collective-permute-start.35 = (bf16[192,384]{1,0:T(8,128)(2,1)S(1)}, bf16[192,384]{1,0:T(8,128)(2,1)S(1)}, u32[]{:S(2)}, u32[]{:S(2)}) collective-permute-start(bf16[192,384]{1,0:T(8,128)(2,1)S(1)} %pad_maximum_fusion.10), channel_id=1, source_target_pairs={{8,0},{16,8},{24,16},{0,24},{9,1},{17,9},{25,17},{1,25},{10,2},{18... | collective-permute-start | bytes 442376 | tf_op jit(solution)/shard_map/ppermute | solution.py:391
  (51 other events, 212.6 us)

commit v2 on v1

--- a/solution.py
+++ b/solution.py
@@ -92,31 +92,50 @@
     return raw, step, decay
 
 
-def proj_columns(proj_ref, width, bc_width):
-    return (
-        proj_ref.at[:, width : 2 * width],
-        proj_ref.at[:, 2 * width : 2 * width + bc_width],
-        proj_ref.at[:, 2 * width + bc_width :],
-    )
-
-
-def forward_kernel(
-    head_dim, proj_ref, xt_ref, bt_ref, heads_ref, y_ref, save_ref, xpad, bpad, state
-):
+def at_rows(index, rows):
+    return pl.ds(pl.multiple_of(index * rows, rows), rows)
+
+
+def forward_kernel(head_dim, dims, idx_ref, *refs):
+    seq, line, parts = dims
+    toks, refs = refs[:seq], refs[seq:]
+    pieces, refs = refs[:parts], refs[parts:]
+    gain_ref, xt_ref, bt_ref, heads_ref, proj_ref, y_ref, save_ref, weight_ref, normed_ref = refs[:9]
+    xpad, bpad, state = refs[9:]
     length, width = y_ref.shape
-    x_ref, bc_ref, dt_ref = proj_columns(proj_ref, width, bt_ref.shape[1])
+    bc_width = bt_ref.shape[1]
+    state_size = bc_width // 2
     head_count = width // head_dim
     per_tile = LANES // head_dim
+    s, p, j = idx_ref[0], idx_ref[1], idx_ref[2]
+    if parts == 1:
+        weight_ref[...] = pieces[0][...]
+    else:
+        shard = pieces[0].shape[0]
+        for k in range(line):
+            at = lax.rem(p + k, line) * 2
+            weight_ref[at_rows(at + j, shard), :] = pieces[k][...]
+            weight_ref[at_rows(at + 1 - j, shard), :] = pieces[line + k][...]
     xpad[0:PAD] = jnp.zeros((PAD, width), F32)
-    bpad[0:PAD] = jnp.zeros((PAD, bc_ref.shape[1]), F32)
-    xpad[PAD:] = x_ref[...].astype(F32)
-    bpad[PAD:] = bc_ref[...].astype(F32)
+    bpad[0:PAD] = jnp.zeros((PAD, bc_width), F32)
+    rows_here = toks[0].shape[0]
+    for k in range(seq):
+        tok = toks[k][...].astype(F32)
+        scale = lax.rsqrt(jnp.mean(tok * tok, axis=1, keepdims=True) + EPSILON)
+        normed = (tok * scale * gain_ref[...]).astype(BF16)
+        start = pl.multiple_of(lax.rem(s + k, seq) * rows_here, rows_here)
+        normed_ref[pl.ds(start, rows_here), :] = normed
+        proj = mm_nn(normed, weight_ref[...]).astype(BF16)
+        proj_ref[pl.ds(start, rows_here), :] = proj
+        padded = pl.multiple_of(start + PAD, PAD)
+        xpad[pl.ds(padded, rows_here), :] = proj[:, width : 2 * width].astype(F32)
+        bpad[pl.ds(padded, rows_here), :] = proj[:, 2 * width : 2 * width + bc_width].astype(F32)
     state[...] = jnp.zeros_like(state)
     row = iota((CHUNK, CHUNK), 0)
     col = iota((CHUNK, CHUNK), 1)
     causal = row >= col
     tril = causal.astype(F32)
-    state_size = bc_ref.shape[1] // 2
+    dt_at = 2 * width + bc_width
 
     def chunk_step(chunk, unused):
         start = pl.multiple_of(chunk * CHUNK, CHUNK)
@@ -126,7 +145,7 @@
         bc = (u_b * sigmoid(u_b)).astype(BF16)
         b, c = bc[:, :state_size], bc[:, state_size:]
         raw, step, decay = decay_terms(
-            dt_ref[pl.ds(start, CHUNK), :].astype(F32), heads_ref[...], tril
+            proj_ref[pl.ds(start, CHUNK), dt_at:].astype(F32), heads_ref[...], tril
         )
         decay_t = jnp.transpose(decay)
         step_t = jnp.transpose(step)
@@ -163,41 +182,154 @@
     lax.fori_loop(0, length // CHUNK, chunk_step, 0)
 
 
-def backward_kernel(
-    head_dim,
-    proj_ref,
-    gy_ref,
-    save_ref,
-    xt_ref,
-    bt_ref,
-    heads_ref,
-    grad_ref,
-    small_x_ref,
-    small_b_ref,
-    small_h_ref,
-    xpad,
-    bpad,
-    dstate,
-    next_x,
-    next_b,
-):
+def gate_terms(proj_ref, y_ref, rows, width):
+    gate = proj_ref[rows, 0:width].astype(F32)
+    ssm = y_ref[rows, :].astype(F32)
+    opened = sigmoid(gate)
+    silu = gate * opened
+    return gate, ssm, opened, silu
+
+
+def stats_kernel(dims, idx_ref, *refs):
+    seq = dims
+    cots, refs = refs[:seq], refs[seq:]
+    out_ref, proj_ref, y_ref, xt_ref, gm_ref, stats_ref = refs
+    width = y_ref.shape[1]
+    rows_here = cots[0].shape[0]
+    s = idx_ref[0]
+    lane = iota((CHUNK, LANES), 1)
+    for k in range(seq):
+        base = lax.rem(s + k, seq) * rows_here
+        grad_mixed = mm_nt(cots[k][...], out_ref[...])
+        gm_ref[pl.ds(pl.multiple_of(base, rows_here), rows_here), :] = grad_mixed
+        for part in range(rows_here // CHUNK):
+            start = pl.multiple_of(base + part * CHUNK, CHUNK)
+            gate, ssm, opened, silu = gate_terms(proj_ref, y_ref, pl.ds(start, CHUNK), width)
+            gated = ssm * silu
+            gained = grad_mixed[part * CHUNK : (part + 1) * CHUNK] * xt_ref[6:7]
+            squares = jnp.sum(gated * gated, axis=1, keepdims=True)
+            cross = jnp.sum(gated * gained, axis=1, keepdims=True)
+            both = jnp.where(lane == 0, squares, jnp.where(lane == 1, cross, 0.0))
+            stats_ref[:, pl.ds(start, CHUNK)] = jnp.transpose(both)[:PAD]
+
+
+def result_kernel(dims, idx_ref, proj_ref, y_ref, xt_ref, out_ref, *parts):
+    seq = dims
+    width = y_ref.shape[1]
+    rows_here = parts[0].shape[0]
+    s = idx_ref[0]
+    for k in range(seq):
+        start = pl.multiple_of(lax.rem(s + seq - k, seq) * rows_here, rows_here)
+        gate, ssm, opened, silu = gate_terms(proj_ref, y_ref, pl.ds(start, rows_here), width)
+        value = (ssm * silu * xt_ref[6:7]).astype(BF16)
+        parts[k][...] = mm_nn(value, out_ref[...]).astype(parts[k].dtype)
+
+
+def gate_kernel(dims, idx_ref, *refs):
+    seq, line, inner, packed = dims
+    cots, refs = refs[:seq], refs[seq:]
+    stats, refs = refs[:seq], refs[seq:]
+    proj_ref, y_ref, gm_ref, xt_ref, normed_ref, gy_ref, gg_ref, gain_part_ref = refs[:8]
+    refs = refs[8:]
+    if packed:
+        keep_ref, send_ref = refs[:2]
+        mixed, gate_w, out_w = refs[2:]
+    else:
+        gate_w, out_w, mixed = refs
+    length, width = y_ref.shape
+    rows_here = cots[0].shape[0]
+    model = normed_ref.shape[1]
+    s, j = idx_ref[0], idx_ref[2]
+    gain = xt_ref[6:7]
+
+    def chunk_step(chunk, total):
+        start = pl.multiple_of(chunk * CHUNK, CHUNK)
+        both = stats[0][:, pl.ds(start, CHUNK)]
+        for k in range(1, seq):
+            both = both + stats[k][:, pl.ds(start, CHUNK)]
+        both = jnp.transpose(jnp.concatenate([both, jnp.zeros((LANES - PAD, CHUNK), F32)], axis=0))
+        scale = lax.rsqrt(both[:, 0:1] / inner + EPSILON)
+        pull = scale * scale * scale * (both[:, 1:2] / inner)
+        rows = pl.ds(start, CHUNK)
+        gate, ssm, opened, silu = gate_terms(proj_ref, y_ref, rows, width)
+        gated = ssm * silu
+        grad_mixed = gm_ref[rows, :]
+        plain = gated * scale
+        mixed[rows, :] = (plain * gain).astype(BF16)
+        grad_gated = scale * (grad_mixed * gain) - gated * pull
+        gy_ref[rows, :] = (grad_gated * silu).astype(BF16)
+        slope = opened * (1.0 + gate * (1.0 - opened))
+        gg_ref[rows, :] = (grad_gated * ssm * slope).astype(BF16)
+        return total + jnp.sum(grad_mixed * plain, axis=0, keepdims=True)
+
+    gain_part_ref[0:1] = lax.fori_loop(0, length // CHUNK, chunk_step, jnp.zeros((1, width), F32))
+
+    gate_w[...] = jnp.zeros_like(gate_w)
+    out_w[...] = jnp.zeros_like(out_w)
+    for k in range(seq):
+        start = pl.multiple_of(lax.rem(s + k, seq) * rows_here, rows_here)
+        rows = pl.ds(start, rows_here)
+        gate_w[...] += mm_tn(normed_ref[rows, :], gg_ref[rows, :])
+        out_w[...] += mm_tn(mixed[rows, :], cots[k][...])
+    if packed:
+        shard = model // (2 * line)
+        piece = width // (2 * line)
+        for p in range(line):
+            for ref, parity in ((keep_ref, j), (send_ref, 1 - j)):
+                at = 2 * p + parity
+                ref[p, 0:shard, :] = gate_w[at_rows(at, shard), :].astype(ref.dtype)
+                for c in range(model // width):
+                    ref[p, shard + c * piece : shard + (c + 1) * piece, :] = out_w[
+                        at_rows(at, piece), c * width : (c + 1) * width
+                    ].astype(ref.dtype)
+
+
+def backward_kernel(head_dim, dims, idx_ref, *refs):
+    seq, line, first, final, packed = dims
+    proj_ref, gy_ref, save_ref, xt_ref, bt_ref, heads_ref = refs[:6]
+    refs = refs[6:]
+    if not first:
+        carried, refs = refs[:7], refs[7:]
+    if final:
+        gg_ref, weight_ref, normed_ref, gain_ref, gain_part_ref = refs[:5]
+        gn_refs, refs = refs[5 : 5 + seq], refs[5 + seq :]
+        if packed:
+            keep_ref, send_ref, small_ref = refs[:3]
+            refs = refs[3:]
+        else:
+            late_w, small_ref = refs[:2]
+            refs = refs[2:]
+        grad_ref, small_x_ref, small_b_ref, small_h_ref, dstate, next_x, next_b = refs[:7]
+        refs = refs[7:]
+        if packed:
+            late_w, refs = refs[0], refs[1:]
+        gn_scratch, xpad, bpad = refs
+    else:
+        grad_ref, small_x_ref, small_b_ref, small_h_ref, dstate, next_x, next_b = refs[:7]
+        xpad, bpad = refs[7:]
     length, width = gy_ref.shape
     bc_width = bt_ref.shape[1]
-    x_ref, bc_ref, dt_ref = proj_columns(proj_ref, width, bc_width)
     state_size = bc_width // 2
     head_count = width // head_dim
     per_tile = LANES // head_dim
     chunks = length // CHUNK
+    half = chunks // 2
+    dt_at = 2 * width + bc_width
     xpad[0:PAD] = jnp.zeros((PAD, width), F32)
     bpad[0:PAD] = jnp.zeros((PAD, bc_width), F32)
-    xpad[PAD:] = x_ref[...].astype(F32)
-    bpad[PAD:] = bc_ref[...].astype(F32)
-    dstate[...] = jnp.zeros_like(dstate)
-    next_x[...] = jnp.zeros_like(next_x)
-    next_b[...] = jnp.zeros_like(next_b)
-    small_x_ref[...] = jnp.zeros_like(small_x_ref)
-    small_b_ref[...] = jnp.zeros_like(small_b_ref)
-    small_h_ref[...] = jnp.zeros_like(small_h_ref)
+    low = 0 if final else half * CHUNK - PAD
+    high = length if first else half * CHUNK
+    xpad[PAD + low : PAD + high] = proj_ref[low:high, width : 2 * width].astype(F32)
+    bpad[PAD + low : PAD + high] = proj_ref[low:high, 2 * width : dt_at].astype(F32)
+    if first:
+        for ref in (small_x_ref, small_b_ref, small_h_ref, dstate, next_x, next_b):
+            ref[...] = jnp.zeros_like(ref)
+    else:
+        for ref, old in zip(
+            (small_x_ref, small_b_ref, small_h_ref, dstate, next_x, next_b), carried[1:]
+        ):
+            ref[...] = old[...]
+        grad_ref[half * CHUNK :, :] = carried[0][half * CHUNK :, :]
     row = iota((CHUNK, CHUNK), 0)
     col = iota((CHUNK, CHUNK), 1)
     causal = row >= col
@@ -227,7 +359,7 @@
         return total
 
     def chunk_step(index, unused):
-        chunk = chunks - 1 - index
+        chunk = (chunks if first else half) - 1 - index
         start = pl.multiple_of(chunk * CHUNK, CHUNK)
         x_rows = xpad[pl.ds(start, CHUNK + PAD), :]
         b_rows = bpad[pl.ds(start, CHUNK + PAD), :]
@@ -237,7 +369,7 @@
         bc = (u_b * sigmoid(u_b)).astype(BF16)
         b, c = bc[:, :state_size], bc[:, state_size:]
         raw, step, decay = decay_terms(
-            dt_ref[pl.ds(start, CHUNK), :].astype(F32), heads_ref[...], tril
+            proj_ref[pl.ds(start, CHUNK), dt_at:].astype(F32), heads_ref[...], tril
         )
         rate = heads_ref[1:2]
         decay_t = jnp.transpose(decay)
@@ -312,61 +444,70 @@
         )
         return unused
 
-    lax.fori_loop(0, chunks, chunk_step, 0)
+    lax.fori_loop(0, chunks - half if first else half, chunk_step, 0)
+    if not final:
+        return
     small_h_ref[2:3] = mm_exact(
         jnp.broadcast_to(small_x_ref[5:6], (PAD, width)), gather_heads
     )[0:1]
-
-
-def scan_forward(head_dim, proj, x_taps, bc_taps, heads):
-    length = proj.shape[0]
-    width, bc_width = x_taps.shape[1], bc_taps.shape[1]
-    state_size = bc_width // 2
-    chunks = length // CHUNK
+    s, j = idx_ref[0], idx_ref[2]
+    model = normed_ref.shape[1]
+    rows_here = gn_refs[0].shape[0]
+    late_width = late_w.shape[1]
+    gain_sum = jnp.zeros((1, model), F32)
+    for k in range(seq):
+        rows = pl.ds(pl.multiple_of(lax.rem(s + seq - k, seq) * rows_here, rows_here), rows_here)
+        gn = mm_nt(gg_ref[rows, :], weight_ref[:, 0:width]) + mm_nt(
+            grad_ref[rows, :], weight_ref[:, width:]
+        )
+        gn_refs[k][...] = gn.astype(gn_refs[k].dtype)
+        gain_sum = gain_sum + jnp.sum(gn * normed_ref[rows, :].astype(F32), axis=0, keepdims=True)
+        late = mm_tn(normed_ref[rows, :], grad_ref[rows, :])
+        late_w[...] = late if k == 0 else late_w[...] + late
+    gain_sum = gain_sum / gain_ref[...]
+    small_ref[...] = jnp.zeros_like(small_ref)
+    small_ref[0:5, 0:width] = small_x_ref[0:5]
+    small_ref[0:5, width : width + bc_width] = small_b_ref[0:5]
+    small_ref[0:3, width + bc_width :] = small_h_ref[0:3]
+    small_ref[5:6, 0:width] = gain_part_ref[0:1]
+    for c in range(0, model, late_width):
+        size = min(late_width, model - c)
+        at = 6 + c // late_width
+        small_ref[at : at + 1, 0:size] = gain_sum[:, c : c + size]
+    if packed:
+        shard = model // (2 * line)
+        for p in range(line):
+            keep_ref[p] = late_w[at_rows(2 * p + j, shard), :]
+            send_ref[p * shard : (p + 1) * shard, :] = late_w[
+                at_rows(2 * p + 1 - j, shard), :
+            ].astype(BF16)
+        high = small_ref[...].astype(BF16)
+        send_ref[line * shard : line * shard + PAD, :] = high
+        send_ref[line * shard + PAD :, :] = (small_ref[...] - high.astype(F32)).astype(BF16)
+
+
+VMEM_SPEC = pl.BlockSpec(memory_space=pltpu.VMEM)
+SMEM_SPEC = pl.BlockSpec(memory_space=pltpu.SMEM)
+
+
+def call(kernel, name, idx, arrays, outs, scratch, flops):
+    bytes_moved = sum(a.size * a.dtype.itemsize for a in list(arrays) + list(outs))
     return pl.pallas_call(
-        functools.partial(forward_kernel, head_dim),
-        out_shape=(
-            jax.ShapeDtypeStruct((length, width), BF16),
-            jax.ShapeDtypeStruct((chunks, state_size, width), BF16),
-        ),
-        scratch_shapes=[
-            pltpu.VMEM((length + PAD, width), F32),
-            pltpu.VMEM((length + PAD, bc_width), F32),
-            pltpu.VMEM((state_size, width), F32),
-        ],
+        kernel,
+        out_shape=tuple(outs),
+        in_specs=[SMEM_SPEC] + [VMEM_SPEC] * len(arrays),
+        out_specs=tuple([VMEM_SPEC] * len(outs)),
+        scratch_shapes=[pltpu.VMEM(*one) for one in scratch],
         compiler_params=pltpu.CompilerParams(vmem_limit_bytes=VMEM_LIMIT),
         cost_estimate=pl.CostEstimate(
-            flops=8 * length * width * CHUNK, bytes_accessed=8 * length * width, transcendentals=0
+            flops=int(flops), bytes_accessed=int(bytes_moved), transcendentals=0
         ),
-        name="scan_forward",
-    )(proj, x_taps, bc_taps, heads)
-
-
-def scan_backward(head_dim, proj, gy, saved, x_taps, bc_taps, heads):
-    length, width = gy.shape
-    bc_width = bc_taps.shape[1]
-    state_size = bc_width // 2
-    return pl.pallas_call(
-        functools.partial(backward_kernel, head_dim),
-        out_shape=(
-            jax.ShapeDtypeStruct((length, width + bc_width + LANES), BF16),
-            jax.ShapeDtypeStruct((PAD, width), F32),
-            jax.ShapeDtypeStruct((PAD, bc_width), F32),
-            jax.ShapeDtypeStruct((PAD, LANES), F32),
-        ),
-        scratch_shapes=[
-            pltpu.VMEM((length + PAD, width), F32),
-            pltpu.VMEM((length + PAD, bc_width), F32),
-            pltpu.VMEM((state_size, width), F32),
-            pltpu.VMEM((PAD, width), F32),
-            pltpu.VMEM((PAD, bc_width), F32),
-        ],
-        compiler_params=pltpu.CompilerParams(vmem_limit_bytes=VMEM_LIMIT),
-        cost_estimate=pl.CostEstimate(
-            flops=24 * length * width * CHUNK, bytes_accessed=16 * length * width, transcendentals=0
-        ),
-        name="scan_backward",
-    )(proj, gy, saved, x_taps, bc_taps, heads)
+        name=name,
+    )(idx, *arrays)
+
+
+def shaped(shape, dtype):
+    return jax.ShapeDtypeStruct(shape, dtype)
 
 
 def put(buffer, value, index, axis=0):
@@ -398,6 +539,12 @@
     def from_sibling(self, value):
         return lax.ppermute(value, "fsdp", [(i ^ 1, i) for i in range(self.fsdp)])
 
+    def parts_seq(self, value):
+        return [value] + [self.from_seq(value, k) for k in range(1, self.seq)]
+
+    def parts_line(self, value):
+        return [value] + [self.from_line(value, k) for k in range(1, self.line)]
+
     def gather_seq(self, value):
         whole = jnp.zeros((self.seq,) + value.shape, value.dtype)
         for k in range(self.seq):
@@ -426,17 +573,22 @@
             ).astype(F32)
         return total
 
-    def sum_fsdp(self, blocks, extra=None):
+    def pair_split(self, blocks, extra=None):
         pairs = blocks.reshape((self.line, 2) + blocks.shape[1:])
-        mine = take(pairs, self.j, 1).astype(F32)
-        other = take(pairs, 1 - self.j, 1).astype(BF16)
+        keep = take(pairs, self.j, 1)
+        send = take(pairs, 1 - self.j, 1).astype(BF16)
         if extra is None:
-            mine = mine + self.from_sibling(other).astype(F32)
+            return keep, send
+        send = send.reshape((-1, send.shape[2]))
+        return keep, jnp.concatenate([send, halves(extra)], axis=0)
+
+    def sum_fsdp(self, keep, send, extra=None):
+        got = self.from_sibling(send)
+        if extra is None:
+            mine = keep + got.astype(F32)
         else:
-            rows = other.shape[0] * other.shape[1]
-            sent = jnp.concatenate([other.reshape((rows,) + other.shape[2:]), halves(extra)], axis=0)
-            got = self.from_sibling(sent)
-            mine = mine + got[:rows].reshape(other.shape).astype(F32)
+            rows = keep.shape[0] * keep.shape[1]
+            mine = keep + got[:rows].reshape(keep.shape).astype(F32)
             extra = extra + whole_of(got[rows:])
         total = take(mine, self.p)
         extra_total = extra
@@ -479,7 +631,8 @@
     cotangent,
 ):
     ring = Ring()
-    s, seq, fsdp = ring.s, ring.seq, ring.fsdp
+    s, seq, fsdp, line = ring.s, ring.seq, ring.fsdp, ring.line
+    idx = jnp.stack([ring.s, ring.p, ring.j]).astype(jnp.int32)
     tok_rows, cot_rows = tokens[0], cotangent[0]
     rows_here, model = tok_rows.shape
     length = rows_here * seq
@@ -489,14 +642,54 @@
     head_dim = inner // all_heads
     heads_here = all_heads // seq
     bc_width = conv_bc_weight.shape[1]
+    state_size = bc_width // 2
     shard = in_weight.shape[0]
     wide = -(-width // LANES) * LANES
+    late_width = wide + bc_width + LANES
+    chunks = length // CHUNK
+    packed = wide == width and shard % 16 == 0 and (width // fsdp) % 16 == 0 and model % width == 0
 
     def columns(array, start, size):
         return lax.dynamic_slice_in_dim(array, start, size, 1)
 
     def pad_lanes(array, value=0.0, size=LANES):
         return jnp.pad(array, ((0, 0), (0, size - array.shape[1])), constant_values=value)
+
+    own_weight = jnp.concatenate(
+        [
+            pad_lanes(columns(in_weight, s * width, width), size=wide),
+            pad_lanes(columns(in_weight, inner + s * width, width), size=wide),
+            in_weight[:, 2 * inner :],
+            pad_lanes(columns(dt_weight, s * heads_here, heads_here)),
+        ],
+        axis=1,
+    )
+    tok_parts = ring.parts_seq(tok_rows)
+    if packed:
+        lane_parts = ring.parts_line(own_weight)
+        pieces = lane_parts + [ring.from_sibling(part) for part in lane_parts]
+    else:
+        pieces = [ring.join_sibling(ring.gather_line(own_weight)).reshape(model, -1)]
+    tok_parts, pieces, cot_rows, out_weight = lax.optimization_barrier(
+        (tok_parts, pieces, cot_rows, out_weight)
+    )
+    cot_parts = ring.parts_seq(cot_rows)
+    out_rows = line // seq
+    out_mine = []
+    for r in range(out_rows):
+        place = s * out_rows + r
+        value = jnp.where(ring.p == place, out_weight, jnp.zeros_like(out_weight))
+        for k in range(1, line):
+            pairs = []
+            for one in range(seq):
+                src = one * out_rows + r
+                dst = (src + k) % line
+                for c in range(2):
+                    pairs.append((one * fsdp + 2 * src + c, one * fsdp + 2 * dst + c))
+            value = value + lax.ppermute(out_weight, ("seq", "fsdp"), pairs)
+        out_mine.append(value)
+    out_here = ring.join_sibling(jnp.stack(out_mine)).reshape(width, model)
+    out_here = jnp.pad(out_here, ((0, wide - width), (0, 0)))
 
     x_taps = columns(
         jnp.concatenate(
@@ -513,7 +706,6 @@
         width,
     )
     x_taps = pad_lanes(x_taps, size=wide)
-    gain = x_taps[6:7]
     bc_taps = jnp.concatenate(
         [conv_bc_weight, conv_bc_bias[None], jnp.zeros((3, bc_width), F32)], axis=0
     )
@@ -522,124 +714,172 @@
     heads = jnp.concatenate(
         [pad_lanes(bias_here, -100.0), pad_lanes(rate_here), jnp.zeros((6, LANES), F32)], axis=0
     )
-
-    own_weight = jnp.concatenate(
+    gain_row = norm_gain[None]
+
+    pads = [((length + PAD, wide), F32), ((length + PAD, bc_width), F32)]
+    projected, ssm_out, saved, weight, normed = call(
+        functools.partial(forward_kernel, head_dim, (seq, line, len(pieces))),
+        "project_scan",
+        idx,
+        tok_parts + pieces + [gain_row, x_taps, bc_taps, heads],
         [
-            pad_lanes(columns(in_weight, s * width, width), size=wide),
-            pad_lanes(columns(in_weight, inner + s * width, width), size=wide),
-            in_weight[:, 2 * inner :],
-            pad_lanes(columns(dt_weight, s * heads_here, heads_here)),
+            shaped((length, wide + late_width), BF16),
+            shaped((length, wide), BF16),
+            shaped((chunks, state_size, wide), BF16),
+            shaped((model, wide + late_width), BF16),
+            shaped((length, model), BF16),
         ],
-        axis=1,
-    )
-    tok_full = ring.gather_seq(tok_rows).reshape(length, model)
-    weight = ring.join_sibling(ring.gather_line(own_weight)).reshape(model, -1)
-    cot_full = ring.gather_seq(cot_rows).reshape(length, model)
-    out_line = ring.gather_line(out_weight)
-    out_rows = ring.line // seq
-    out_here = lax.dynamic_slice_in_dim(out_line, s * out_rows, out_rows, 0)
-    out_here = ring.join_sibling(out_here).reshape(width, model)
-    out_here = jnp.pad(out_here, ((0, wide - width), (0, 0)))
-
-    def rms(rows):
-        return lax.rsqrt(jnp.mean(rows * rows, axis=-1, keepdims=True) + EPSILON)
-
-    tok_wide = tok_full.astype(F32)
-    scaled = tok_wide * rms(tok_wide)
-    normed = (scaled * norm_gain).astype(BF16)
-    projected = mm_nn(normed, weight).astype(BF16)
-    ssm_out, saved = scan_forward(head_dim, projected, x_taps, bc_taps, heads)
-    grad_mixed = mm_nt(cot_full, out_here)
-    gate = projected[:, :wide].astype(F32)
-    ssm = ssm_out.astype(F32)
-    opened = jax.nn.sigmoid(gate)
-    silu = gate * opened
-    gated = ssm * silu
-    gained = grad_mixed * gain
-    stats = jnp.stack([jnp.sum(gated * gated, axis=1), jnp.sum(gated * gained, axis=1)])
-    stats = stats + sum(ring.from_seq(stats, k) for k in range(1, seq))
-    scale = lax.rsqrt(stats[0] / inner + EPSILON)[:, None]
-    pull = (scale * scale * scale) * (stats[1][:, None] / inner)
-    mixed_plain = gated * scale
-    mixed = (mixed_plain * gain).astype(BF16)
-    grad_gated = scale * gained - gated * pull
-    grad_ssm = (grad_gated * silu).astype(BF16)
-    grad_gate = (grad_gated * ssm * (opened * (1.0 + gate * (1.0 - opened)))).astype(BF16)
-    gate_gain_part = jnp.sum(grad_mixed * mixed_plain, axis=0)
-
-    out_part = mm_nn(mixed, out_here).astype(BF16).reshape(seq, rows_here, model)
-    result = tok_rows.astype(F32) + ring.sum_seq(out_part)
-
-    gate_weight_part = mm_tn(normed, grad_gate)[:, :width].reshape(fsdp, shard, width)
-    out_weight_part = mm_tn(mixed, cot_full)[:width].reshape(fsdp, width // fsdp, model)
-    early = jnp.concatenate(
-        [gate_weight_part]
-        + [out_weight_part[:, :, c : c + width] for c in range(0, model, width)],
-        axis=1,
-    )
-    early, unused = ring.sum_fsdp(early)
-    total = seq * fsdp
+        pads + [((state_size, wide), F32)],
+        8 * length * wide * CHUNK,
+    )
+    grad_mixed, stats = call(
+        functools.partial(stats_kernel, seq),
+        "gate_stats",
+        idx,
+        cot_parts + [out_here, projected, ssm_out, x_taps],
+        [shaped((length, wide), F32), shaped((PAD, length), F32)],
+        [],
+        2 * length * wide * model,
+    )
+    stat_parts = ring.parts_seq(stats)
+    out_parts = call(
+        functools.partial(result_kernel, seq),
+        "out_project",
+        idx,
+        [projected, ssm_out, x_taps, out_here],
+        [shaped((rows_here, model), F32 if k == 0 else BF16) for k in range(seq)],
+        [],
+        2 * length * wide * model,
+    )
+    out_sum = out_parts[0]
+    for k in range(1, seq):
+        out_sum = out_sum + ring.from_seq(out_parts[k], k).astype(F32)
+
+    extra_rows = (width // fsdp) * (model // width)
+    grid_w = ((model, wide), F32), ((wide, model), F32), ((length, wide), BF16)
+    if packed:
+        outs = [
+            shaped((line, shard + extra_rows, width), F32),
+            shaped((line, shard + extra_rows, width), BF16),
+        ]
+        scratch = [grid_w[2], grid_w[0], grid_w[1]]
+    else:
+        outs = [shaped(*grid_w[0]), shaped(*grid_w[1])]
+        scratch = [grid_w[2]]
+    grad_ssm, grad_gate, gain_part, one, two = call(
+        functools.partial(gate_kernel, (seq, line, inner, packed)),
+        "gate_backward",
+        idx,
+        cot_parts + stat_parts + [projected, ssm_out, grad_mixed, x_taps, normed],
+        [
+            shaped((length, wide), BF16),
+            shaped((length, wide), BF16),
+            shaped((PAD, wide), F32),
+        ]
+        + outs,
+        scratch,
+        4 * length * wide * model,
+    )
+    if packed:
+        keep, send = one, two
+    else:
+        out_blocks = two[:width].reshape(fsdp, width // fsdp, model)
+        keep, send = ring.pair_split(
+            jnp.concatenate(
+                [one[:, :width].reshape(fsdp, shard, width)]
+                + [out_blocks[:, :, c : c + width] for c in range(0, model, width)],
+                axis=1,
+            )
+        )
+    early, unused = ring.sum_fsdp(keep, send)
     out_block = lax.ppermute(
         early[shard:].astype(BF16),
         ("seq", "fsdp"),
-        [(k, (k % seq) * fsdp + k // seq) for k in range(total)],
+        [(k, (k % seq) * fsdp + k // seq) for k in range(seq * fsdp)],
     )
     early = ring.gather_seq(jnp.concatenate([early[:shard].astype(BF16), out_block], axis=0))
     gate_weight_grad = early[:, :shard]
     out_weight_grad = early[:, shard:].reshape(seq, model // width, width // fsdp, width)
     out_weight_grad = out_weight_grad.transpose(0, 2, 1, 3).reshape(-1, model).astype(F32)
 
-    grad_cols, small_x, small_bc, small_heads = scan_backward(
-        head_dim, projected, grad_ssm, saved, x_taps, bc_taps, heads
-    )
-    gn_part = mm_nt(grad_gate, weight[:, :wide]) + mm_nt(grad_cols, weight[:, wide:])
-    norm_gain_part = jnp.sum(gn_part * scaled, axis=0)
-    grad_normed = ring.sum_seq(gn_part.astype(BF16).reshape(seq, rows_here, model))
-    late_part = mm_tn(normed, grad_cols).reshape(fsdp, shard, -1)
-    late_width = late_part.shape[2]
-
-    pieces = [
-        norm_gain_part,
-        gate_gain_part[:width],
-        small_x[:5, :width].reshape(-1),
-        small_bc[:5].reshape(-1),
-        small_heads[:3, :heads_here].reshape(-1),
+    stats_here = lax.dynamic_slice_in_dim(sum(stat_parts)[0], s * rows_here, rows_here, 0)
+    out_scale = lax.rsqrt(stats_here / inner + EPSILON)[:, None]
+    result = tok_rows.astype(F32) + out_sum * out_scale
+
+    base = [projected, grad_ssm, saved, x_taps, bc_taps, heads]
+    state_outs = [
+        shaped((length, late_width), BF16),
+        shaped((PAD, wide), F32),
+        shaped((PAD, bc_width), F32),
+        shaped((PAD, LANES), F32),
+        shaped((state_size, wide), F32),
+        shaped((PAD, wide), F32),
+        shaped((PAD, bc_width), F32),
     ]
-    sizes = [piece.shape[0] for piece in pieces]
-    flat = jnp.concatenate(pieces)
-    small_rows = -(-flat.shape[0] // (8 * late_width)) * 8
-    flat = jnp.pad(flat, (0, small_rows * late_width - flat.shape[0]))
-    late, small = ring.sum_fsdp(late_part, flat.reshape(small_rows, late_width))
+    carried = call(
+        functools.partial(backward_kernel, head_dim, (seq, line, True, False, packed)),
+        "scan_back_late",
+        idx,
+        base,
+        state_outs,
+        pads,
+        12 * length * wide * CHUNK,
+    )
+    small_shape = ((PAD, late_width), F32)
+    late_shape = ((model, late_width), F32)
+    if packed:
+        outs = [
+            shaped((line, shard, late_width), F32),
+            shaped((line * shard + 2 * PAD, late_width), BF16),
+            shaped(*small_shape),
+        ]
+        scratch = [(o.shape, o.dtype) for o in state_outs] + [late_shape]
+    else:
+        outs = [shaped(*late_shape), shaped(*small_shape)]
+        scratch = [(o.shape, o.dtype) for o in state_outs]
+    done = call(
+        functools.partial(backward_kernel, head_dim, (seq, line, False, True, packed)),
+        "scan_back_early",
+        idx,
+        base + list(carried) + [grad_gate, weight, normed, gain_row, gain_part],
+        [shaped((rows_here, model), F32 if k == 0 else BF16) for k in range(seq)] + outs,
+        scratch + [((PAD, LANES), F32)] + pads,
+        12 * length * wide * CHUNK + 4 * length * model * late_width,
+    )
+    gn_parts, done = done[:seq], done[seq:]
+    grad_normed = gn_parts[0]
+    for k in range(1, seq):
+        grad_normed = grad_normed + ring.from_seq(gn_parts[k], k).astype(F32)
+    if packed:
+        keep, send, small = done
+    else:
+        late_part, small = done
+        keep, send = ring.pair_split(late_part.reshape(fsdp, shard, late_width), small)
+    late, small = ring.sum_fsdp(keep, send, small)
     late = ring.gather_seq(jnp.concatenate([late.astype(BF16), halves(small)], axis=0))
-    small = (
-        late[:, shard : shard + small_rows].astype(F32) + late[:, shard + small_rows :].astype(F32)
-    ).reshape(seq, -1)
-    parts = []
-    at = 0
-    for size in sizes:
-        parts.append(small[:, at : at + size])
-        at += size
-    norm_gain_grad = parts[0].sum(0)
-    gate_gain_grad = parts[1].reshape(-1)
-    conv_x = parts[2].reshape(seq, 5, width).transpose(1, 0, 2).reshape(5, inner)
-    conv_bc = parts[3].sum(0).reshape(5, bc_width)
-    head_grads = parts[4].reshape(seq, 3, heads_here).transpose(1, 0, 2).reshape(3, all_heads)
+    small = late[:, shard : shard + PAD].astype(F32) + late[:, shard + PAD :].astype(F32)
+    head_at = wide + bc_width
+    conv_x = small[:, :5, :width].transpose(1, 0, 2).reshape(5, inner)
+    conv_bc = small[:, :5, wide:head_at].sum(0)
+    head_grads = small[:, :3, head_at : head_at + heads_here].transpose(1, 0, 2)
+    head_grads = head_grads.reshape(3, all_heads)
+    gate_gain_grad = small[:, 5, :width].reshape(-1)
+    norm_gain_grad = small[:, 6:].sum(0).reshape(-1)[:model]
 
     late = late[:, :shard].astype(F32)
     in_weight_grad = jnp.concatenate(
         [
             gate_weight_grad.astype(F32).transpose(1, 0, 2).reshape(shard, inner),
             late[:, :, :width].transpose(1, 0, 2).reshape(shard, inner),
-            late[:, :, wide : wide + bc_width].sum(0),
+            late[:, :, wide:head_at].sum(0),
         ],
         axis=1,
     )
-    dt_at = wide + bc_width
-    dt_weight_grad = late[:, :, dt_at : dt_at + heads_here].transpose(1, 0, 2)
+    dt_weight_grad = late[:, :, head_at : head_at + heads_here].transpose(1, 0, 2)
     dt_weight_grad = dt_weight_grad.reshape(shard, all_heads)
 
     tok_wide = tok_rows.astype(F32)
-    scale = rms(tok_wide)
+    scale = lax.rsqrt(jnp.mean(tok_wide * tok_wide, axis=-1, keepdims=True) + EPSILON)
     gained = grad_normed * norm_gain
     grad_tok = scale * gained - tok_wide * (
         scale * scale * scale * jnp.mean(gained * tok_wide, axis=-1, keepdims=True)

time: 246 us -> 243 us (0.988)
  Pallas kernels: 33.3 us -> 64.1 us
  matrix products: 22.8 us -> 0 us
  other arithmetic: 15 us -> 7.86 us
  waiting for transfers between devices: 76.5 us -> 81.3 us
  starting transfers between devices: 55.8 us -> 51.9 us
  local copies, waits for them, and re-layouts: 39.6 us -> 36 us
    pallas_call x2 -> x6, Pallas kernels: 33.3 us -> 64.1 us  [call(): pl.pallas_call(kernel, out_shape=tuple(outs), in_specs=[SMEM_SPEC] + [VME...]
    dot_general x8 -> x0, matrix products: 22.8 us -> none  [mm(): lax.dot_general(left, right, (dims, ((), ())), preferred_element_type=F32)]
    dynamic_update_slice x25 -> x8, local copies, waits for them, and re-layouts: 4.64 us -> 19.1 us  [put(): return lax.dynamic_update_index_in_dim(buffer, value, index, axis)]
    ppermute x0 -> x3, waiting for transfers between devices: none -> 11.7 us  [local(): value = value + lax.ppermute(out_weight, ('seq', 'fsdp'), pairs)]
    ppermute x12 -> x9, starting transfers between devices: 26.1 us -> 18.6 us  [from_line(): return lax.ppermute(value, 'fsdp', pairs)]
    unnamed x97 -> x75, local copies, waits for them, and re-layouts: 12.6 us -> 5.27 us
    ppermute x12 -> x9, waiting for transfers between devices: 38.3 us -> 32.7 us  [from_line(): return lax.ppermute(value, 'fsdp', pairs)]
    ppermute x0 -> x3, starting transfers between devices: none -> 5.16 us  [local(): value = value + lax.ppermute(out_weight, ('seq', 'fsdp'), pairs)]
  transfers between devices with their start and end apart: 38 -> 41, of which waited for: 15 -> 17; matrix products, arithmetic and copies ran while one was open for 13% -> 15% of each run, Pallas kernels for 0% -> 8%
where the time goes in v2:
time: 243 us
  waiting for transfers between devices  81.3 us (33%)
  Pallas kernels  64.1 us (26%)
  starting transfers between devices  51.9 us (21%)
  local copies, waits for them, and re-layouts  36 us (15%)
  other arithmetic  7.86 us (3%)
    pallas_call x6, Pallas kernels, call(): pl.pallas_call(kernel, out_shape=tuple(outs), in_specs=[SMEM_SPEC] + [VME...  64.1 us
    ppermute x21, waiting for transfers between devices, from_seq(): return lax.ppermute(value, 'seq', [((i + k) % n, i) for i in range(n)])  36.8 us
    ppermute x9, waiting for transfers between devices, from_line(): return lax.ppermute(value, 'fsdp', pairs)  32.7 us
    ppermute x21, starting transfers between devices, from_seq(): return lax.ppermute(value, 'seq', [((i + k) % n, i) for i in range(n)])  26.9 us
    dynamic_update_slice x8, local copies, waits for them, and re-layouts, put(): return lax.dynamic_update_index_in_dim(buffer, value, index, axis)  19.1 us
    ppermute x9, starting transfers between devices, from_line(): return lax.ppermute(value, 'fsdp', pairs)  18.6 us
    ppermute x3, waiting for transfers between devices, local(): value = value + lax.ppermute(out_weight, ('seq', 'fsdp'), pairs)  11.7 us
    unnamed x75, local copies, waits for them, and re-layouts  5.27 us
  transfers between devices with their start and end apart: 41, of which 17 were waited for; matrix products, arithmetic and copies ran while one was open for 15% of the time, Pallas kernels for 8%

profile of v2, /device:TPU:0, one launch (start us, length us, event | category | flops | bytes accessed | tf_op | source)
XLA Modules:
  0.0 242.6 jit_solution(13980324831120285834)
XLA Ops:
  3.3 5.1 %collective-permute-start.3 = (bf16[96,1152]{1,0:T(8,128)(2,1)S(1)}, bf16[96,1152]{1,0:T(8,128)(2,1)S(1)}, u32[]{:S(2)}, u32[]{:S(2)}) collective-permute-start(bf16[96,1152]{1,0:T(8,128)(2,1)S(1)} %fusion.13.refs_4_), channel_id=1, source_target_pairs={{2,0},{3,1},{4,2},{5,3},{6,4},{7,5},{0,6},{1,7},{10,8},{11,9},{12,... | collective-permute-start | bytes 663560 | tf_op jit(solution)/shard_map/ppermute | solution.py:537
  8.4 2.4 %collective-permute-start = (bf16[256,768]{1,0:T(8,128)(2,1)}, bf16[256,768]{1,0:T(8,128)(2,1)S(1)}, u32[]{:S(2)}, u32[]{:S(2)}) collective-permute-start(bf16[256,768]{1,0:T(8,128)(2,1)} %bitcast.104), channel_id=1, source_target_pairs={{8,0},{16,8},{24,16},{0,24},{9,1},{17,9},{25,17},{1,25},{10,2},{18... | collective-permute-start | bytes 1179656 | tf_op jit(solution)/shard_map/ppermute | solution.py:532
  11.9 2.4 collective-permute-done.3.refs_5_
  15.8 11.4 %collective-permute-done.4.refs_6_ = bf16[96,1152]{1,0:T(8,128)(2,1)S(1)} collective-permute-done((bf16[96,1152]{1,0:T(8,128)(2,1)S(1)}, bf16[96,1152]{1,0:T(8,128)(2,1)S(1)}, u32[]{:S(2)}, u32[]{:S(2)}) %collective-permute-start.4) | collective-permute-done | bytes 221216 | tf_op jit(solution)/shard_map/ppermute | solution.py:537
  29.5 8.8 %collective-permute-done.2.refs_3_ = bf16[256,768]{1,0:T(8,128)(2,1)S(1)} collective-permute-done((bf16[256,768]{1,0:T(8,128)(2,1)}, bf16[256,768]{1,0:T(8,128)(2,1)S(1)}, u32[]{:S(2)}, u32[]{:S(2)}) %collective-permute-start.2) | collective-permute-done | bytes 393248 | tf_op jit(solution)/shard_map/ppermute | solution.py:532
  39.0 2.5 %collective-permute-start.10 = (bf16[192,768]{1,0:T(8,128)(2,1)}, bf16[192,768]{1,0:T(8,128)(2,1)S(1)}, u32[]{:S(2)}, u32[]{:S(2)}) collective-permute-start(bf16[192,768]{1,0:T(8,128)(2,1)} %param.26), channel_id=1, source_target_pairs={{0,2},{1,3},{10,12},{11,13},{20,22},{21,23},{30,24},{31,25}} | collective-permute-start | bytes 884744 | tf_op jit(solution)/shard_map/ppermute | solution.py:689
  46.4 2.9 %collective-permute-done.10 = bf16[192,768]{1,0:T(8,128)(2,1)S(1)} collective-permute-done((bf16[192,768]{1,0:T(8,128)(2,1)}, bf16[192,768]{1,0:T(8,128)(2,1)S(1)}, u32[]{:S(2)}, u32[]{:S(2)}) %collective-permute-start.10) | collective-permute-done | bytes 294944 | tf_op jit(solution)/shard_map/ppermute | solution.py:689
  49.3 5.7 %collective-permute-done.11 = bf16[192,768]{1,0:T(8,128)(2,1)S(1)} collective-permute-done((bf16[192,768]{1,0:T(8,128)(2,1)}, bf16[192,768]{1,0:T(8,128)(2,1)S(1)}, u32[]{:S(2)}, u32[]{:S(2)}) %collective-permute-start.11) | collective-permute-done | bytes 294944 | tf_op jit(solution)/shard_map/ppermute | solution.py:689
  54.9 3.2 %collective-permute-done.12 = bf16[192,768]{1,0:T(8,128)(2,1)S(1)} collective-permute-done((bf16[192,768]{1,0:T(8,128)(2,1)}, bf16[192,768]{1,0:T(8,128)(2,1)S(1)}, u32[]{:S(2)}, u32[]{:S(2)}) %collective-permute-start.12) | collective-permute-done | bytes 294944 | tf_op jit(solution)/shard_map/ppermute | solution.py:689
  59.1 2.0 collective-permute-start.19
  63.2 14.3 %project_scan.1 = (bf16[1024,1152]{1,0:T(8,128)(2,1)}, bf16[1024,384]{1,0:T(8,128)(2,1)}, bf16[8,128,384]{2,1,0:T(8,128)(2,1)}, bf16[768,1152]{1,0:T(8,128)(2,1)}, bf16[1024,768]{1,0:T(8,128)(2,1)}) custom-call(s32[3]{0:T(128)} %pad_add_fusion.idx_ref, bf16[256,768]{1,0:T(8,128)(2,1)} %bitcast.107, bf16[256,768]{1,0:T(8,128)(2,1)} %copy-done.13, ...), custom_call_target="tpu_custom_call" | custom-call | flops 402653184 | bytes 10644480 | tf_op jit(solution)/shard_map/project_scan/pallas_call | solution.py:495
  80.0 5.1 %gate_stats.1 = (f32[1024,384]{1,0:T(8,128)}, f32[8,1024]{1,0:T(8,128)}) custom-call(s32[3]{0:T(128)} %pad_add_fusion.idx_ref, bf16[256,768]{1,0:T(8,128)(2,1)} %bitcast.98, bf16[256,768]{1,0:T(8,128)(2,1)} %copy-done.6, bf16[256,768]{1,0:T(8,128)(2,1)} %copy-done.7, bf16[256,768]{1,0:T(8,128)(2,1)} %copy-done.8, bf16[384,768]{1,0:T(8,128)(2,1)} %bitcast.96, ...), custom_call_target="tpu_custom_call" | custom-call | flops 603979776 | bytes 6926336 | tf_op jit(solution)/shard_map/gate_stats/pallas_call | solution.py:495
  92.4 9.0 %gate_backward.1 = (bf16[1024,384]{1,0:T(8,128)(2,1)}, bf16[1024,384]{1,0:T(8,128)(2,1)}, f32[8,384]{1,0:T(8,128)}, f32[4,192,384]{2,1,0:T(8,128)}, bf16[4,192,384]{2,1,0:T(8,128)(2,1)}) custom-call(s32[3]{0:T(128)} %pad_add_fusion.idx_ref, bf16[256,768]{1,0:T(8,128)(2,1)} %bitcast.99, bf16[256,768]{1,0:T(8,128)(2,1)} %copy-done.6, ...), custom_call_target="tpu_custom_call" | custom-call | flops 1207959552 | bytes 11362304 | tf_op jit(solution)/shard_map/gate_backward/pallas_call | solution.py:495
  101.3 13.0 %scan_back_late.1 = (bf16[1024,768]{1,0:T(8,128)(2,1)}, f32[8,384]{1,0:T(8,128)}, f32[8,256]{1,0:T(8,128)}, f32[8,128]{1,0:T(8,128)}, f32[128,384]{1,0:T(8,128)}, /*index=5*/f32[8,384]{1,0:T(8,128)}, f32[8,256]{1,0:T(8,128)}) custom-call(s32[3]{0:T(128)} %pad_add_fusion.idx_ref, bf16[1024,1152]{1,0:T(8,128)(2,1)} %get-tuple-element.70.proj_ref.refs_5_.refs_8_.refs_0_, ...), custom_call_target="tpu_custom_call" | custom-call | flops 603979776 | bytes 5771264 | tf_op jit(solution)/shard_map/scan_back_late/pallas_call | solution.py:495
  114.3 18.8 %scan_back_early.1 = (f32[256,768]{1,0:T(8,128)}, bf16[256,768]{1,0:T(8,128)(2,1)}, bf16[256,768]{1,0:T(8,128)(2,1)}, bf16[256,768]{1,0:T(8,128)(2,1)}, f32[4,96...) custom-call(s32[3]{0:T(128)} %pad_add_fusion.idx_ref, ...), custom_call_target="tpu_custom_call" | custom-call | flops 3019898880 | bytes 13700096 | tf_op jit(solution)/shard_map/scan_back_early/pallas_call | solution.py:495
  137.6 4.0 %out_project.1 = (f32[256,768]{1,0:T(8,128)}, bf16[256,768]{1,0:T(8,128)(2,1)}, bf16[256,768]{1,0:T(8,128)(2,1)}, bf16[256,768]{1,0:T(8,128)(2,1)}) custom-call(s32[3]{0:T(128)} %pad_add_fusion.idx_ref, bf16[1024,1152]{1,0:T(8,128)(2,1)} %get-tuple-element.70.proj_ref.refs_5_.refs_8_.refs_0_, bf16[1024,384]{1,0:T(8,128)(2,1)} %get-tuple-element.71.y_ref.refs_6_.refs_9_, ...), custom_call_target="tpu_custom_call" | custom-call | flops 603979776 | bytes 5713920 | tf_op jit(solution)/shard_map/out_project/pallas_call | solution.py:495
  147.0 4.2 %collective-permute-done.24 = bf16[256,768]{1,0:T(8,128)(2,1)S(1)} collective-permute-done((bf16[256,768]{1,0:T(8,128)(2,1)}, bf16[256,768]{1,0:T(8,128)(2,1)S(1)}, u32[]{:S(2)}, u32[]{:S(2)}) %collective-permute-start.24) | collective-permute-done | bytes 393248 | tf_op jit(solution)/shard_map/ppermute | solution.py:532
  151.2 3.6 %collective-permute-done.25 = bf16[256,768]{1,0:T(8,128)(2,1)S(1)} collective-permute-done((bf16[256,768]{1,0:T(8,128)(2,1)}, bf16[256,768]{1,0:T(8,128)(2,1)S(1)}, u32[]{:S(2)}, u32[]{:S(2)}) %collective-permute-start.25) | collective-permute-done | bytes 393248 | tf_op jit(solution)/shard_map/ppermute | solution.py:532
  155.3 7.0 %collective-permute-done.14 = bf16[256,768]{1,0:T(8,128)(2,1)S(1)} collective-permute-done((bf16[256,768]{1,0:T(8,128)(2,1)}, bf16[256,768]{1,0:T(8,128)(2,1)S(1)}, u32[]{:S(2)}, u32[]{:S(2)}) %collective-permute-start.14) | collective-permute-done | bytes 393248 | tf_op jit(solution)/shard_map/ppermute | solution.py:532
  162.3 6.8 %collective-permute-done.16 = bf16[256,768]{1,0:T(8,128)(2,1)S(1)} collective-permute-done((bf16[256,768]{1,0:T(8,128)(2,1)}, bf16[256,768]{1,0:T(8,128)(2,1)S(1)}, u32[]{:S(2)}, u32[]{:S(2)}) %collective-permute-start.16) | collective-permute-done | bytes 393248 | tf_op jit(solution)/shard_map/ppermute | solution.py:532
  171.0 5.0 %collective-permute-start.34 = (bf16[192,384]{1,0:T(8,128)(2,1)S(1)}, bf16[192,384]{1,0:T(8,128)(2,1)S(1)}, u32[]{:S(2)}, u32[]{:S(2)}) collective-permute-start(bf16[192,384]{1,0:T(8,128)(2,1)S(1)} %get-tuple-element.108), channel_id=1, source_target_pairs={{2,0},{3,1},{4,2},{5,3},{6,4},{7,5},{0,6},{1,7},{10,8},{11,9},{12,... | collective-permute-start | bytes 442376 | tf_op jit(solution)/shard_map/ppermute | solution.py:537
  177.0 1.9 collective-permute-start.36
  179.8 1.9 collective-permute-start.27
  181.9 2.4 collective-permute-start.29
  184.3 14.5 %collective-permute-done.35 = bf16[192,384]{1,0:T(8,128)(2,1)S(1)} collective-permute-done((bf16[192,384]{1,0:T(8,128)(2,1)S(1)}, bf16[192,384]{1,0:T(8,128)(2,1)S(1)}, u32[]{:S(2)}, u32[]{:S(2)}) %collective-permute-start.35) | collective-permute-done | bytes 147488 | tf_op jit(solution)/shard_map/ppermute | solution.py:537
  199.6 4.5 %collective-permute-done.28 = bf16[112,768]{1,0:T(8,128)(2,1)S(1)} collective-permute-done((bf16[112,768]{1,0:T(8,128)(2,1)S(1)}, bf16[112,768]{1,0:T(8,128)(2,1)S(1)}, u32[]{:S(2)}, u32[]{:S(2)}) %collective-permute-start.28) | collective-permute-done | bytes 172064 | tf_op jit(solution)/shard_map/ppermute | solution.py:537
  206.1 2.9 %collective-permute-start.31 = (bf16[112,768]{1,0:T(8,128)(2,1)S(1)}, bf16[112,768]{1,0:T(8,128)(2,1)S(1)}, u32[]{:S(2)}, u32[]{:S(2)}) collective-permute-start(bf16[112,768]{1,0:T(8,128)(2,1)S(1)} %get-tuple-element.122), channel_id=1, source_target_pairs={{16,0},{24,8},{0,16},{8,24},{17,1},{25,9},{1,17},{9,25},{18,2},{26... | collective-permute-start | bytes 516104 | tf_op jit(solution)/shard_map/ppermute | solution.py:532
  209.5 4.8 %dynamic_update_slice.35 = bf16[4,112,768]{2,0,1:T(4,128)(2,1)S(1)} dynamic-update-slice(bf16[4,112,768]{2,0,1:T(4,128)(2,1)S(1)} %broadcast_in_dim.95, bf16[1,112,768]{2,0,1:T(2,128)(2,1)S(1)} %copy.44, s32[]{:T(128)S(6)} %select_n.140, s32[]{:T(128)} %constant.154.clone.1, s32[]{:T(128)} %constant.154.clone.1) | dynamic-update-slice | bytes 344068 | tf_op jit(solution)/shard_map/jit(dynamic_update_index_in_dim)/dynamic_update_slice | solution.py:514
  214.3 3.0 %collective-permute-start.38 = (bf16[192,384]{1,0:T(8,128)(2,1)S(1)}, bf16[192,384]{1,0:T(8,128)(2,1)S(1)}, u32[]{:S(2)}, u32[]{:S(2)}) collective-permute-start(bf16[192,384]{1,0:T(8,128)(2,1)S(1)} %pad_maximum_fusion.8), channel_id=1, source_target_pairs={{8,0},{16,8},{24,16},{0,24},{9,1},{17,9},{25,17},{1,25},{10,2},{18... | collective-permute-start | bytes 442376 | tf_op jit(solution)/shard_map/ppermute | solution.py:532
  218.9 4.8 %dynamic_update_slice.36 = bf16[4,112,768]{2,0,1:T(4,128)(2,1)S(1)} dynamic-update-slice(bf16[4,112,768]{2,0,1:T(4,128)(2,1)S(1)} %dynamic_update_slice.35, bf16[1,112,768]{2,0,1:T(2,128)(2,1)S(1)} %copy.45, s32[]{:T(128)S(6)} %select_n.142, s32[]{:T(128)} %constant.154.clone.1, s32[]{:T(128)} %constant.154.clone.1) | dynamic-update-slice | bytes 344068 | tf_op jit(solution)/shard_map/jit(dynamic_update_index_in_dim)/dynamic_update_slice | solution.py:514
  223.7 4.8 %dynamic_update_slice.37 = bf16[4,112,768]{2,0,1:T(4,128)(2,1)S(1)} dynamic-update-slice(bf16[4,112,768]{2,0,1:T(4,128)(2,1)S(1)} %dynamic_update_slice.36, bf16[1,112,768]{2,0,1:T(2,128)(2,1)S(1)} %copy.46, s32[]{:T(128)S(6)} %select_n.144, s32[]{:T(128)} %constant.154.clone.1, s32[]{:T(128)} %constant.154.clone.1) | dynamic-update-slice | bytes 344068 | tf_op jit(solution)/shard_map/jit(dynamic_update_index_in_dim)/dynamic_update_slice | solution.py:514
  228.4 4.8 %dynamic_update_slice.38 = bf16[4,112,768]{2,0,1:T(4,128)(2,1)S(1)} dynamic-update-slice(bf16[4,112,768]{2,0,1:T(4,128)(2,1)S(1)} %dynamic_update_slice.37, bf16[1,112,768]{2,0,1:T(2,128)(2,1)S(1)} %copy.47, s32[]{:T(128)S(6)} %select_n.146, s32[]{:T(128)} %constant.154.clone.1, s32[]{:T(128)} %constant.154.clone.1) | dynamic-update-slice | bytes 344068 | tf_op jit(solution)/shard_map/jit(dynamic_update_index_in_dim)/dynamic_update_slice | solution.py:514
  (220 shorter events, 53.8 us)
Async XLA Ops:
  3.3 10.9 %collective-permute-start.3 = (bf16[96,1152]{1,0:T(8,128)(2,1)S(1)}, bf16[96,1152]{1,0:T(8,128)(2,1)S(1)}, u32[]{:S(2)}, u32[]{:S(2)}) collective-permute-start(bf16[96,1152]{1,0:T(8,128)(2,1)S(1)} %fusion.13.refs_4_), channel_id=1, source_target_pairs={{2,0},{3,1},{4,2},{5,3},{6,4},{7,5},{0,6},{1,7},{10,8},{11,9},{12,... | collective-permute-start | bytes 663560 | tf_op jit(solution)/shard_map/ppermute | solution.py:537
  8.4 18.8 %collective-permute-start.4 = (bf16[96,1152]{1,0:T(8,128)(2,1)S(1)}, bf16[96,1152]{1,0:T(8,128)(2,1)S(1)}, u32[]{:S(2)}, u32[]{:S(2)}) collective-permute-start(bf16[96,1152]{1,0:T(8,128)(2,1)S(1)} %fusion.13.refs_4_), channel_id=1, source_target_pairs={{4,0},{5,1},{6,2},{7,3},{0,4},{1,5},{2,6},{3,7},{12,8},{13,9},{14,... | collective-permute-start | bytes 663560 | tf_op jit(solution)/shard_map/ppermute | solution.py:537
  8.4 20.8 %collective-permute-start = (bf16[256,768]{1,0:T(8,128)(2,1)}, bf16[256,768]{1,0:T(8,128)(2,1)S(1)}, u32[]{:S(2)}, u32[]{:S(2)}) collective-permute-start(bf16[256,768]{1,0:T(8,128)(2,1)} %bitcast.104), channel_id=1, source_target_pairs={{8,0},{16,8},{24,16},{0,24},{9,1},{17,9},{25,17},{1,25},{10,2},{18... | collective-permute-start | bytes 1179656 | tf_op jit(solution)/shard_map/ppermute | solution.py:532
  10.8 17.8 %collective-permute-start.5 = (bf16[96,1152]{1,0:T(8,128)(2,1)S(1)}, bf16[96,1152]{1,0:T(8,128)(2,1)S(1)}, u32[]{:S(2)}, u32[]{:S(2)}) collective-permute-start(bf16[96,1152]{1,0:T(8,128)(2,1)S(1)} %fusion.13.refs_4_), channel_id=1, source_target_pairs={{6,0},{7,1},{0,2},{1,3},{2,4},{3,5},{4,6},{5,7},{14,8},{15,9},{8,1... | collective-permute-start | bytes 663560 | tf_op jit(solution)/shard_map/ppermute | solution.py:537
  11.9 16.8 %collective-permute-start.6 = (bf16[96,1152]{1,0:T(8,128)(2,1)S(1)}, bf16[96,1152]{1,0:T(8,128)(2,1)S(1)}, u32[]{:S(2)}, u32[]{:S(2)}) collective-permute-start(bf16[96,1152]{1,0:T(8,128)(2,1)S(1)} %fusion.13.refs_4_), channel_id=1, source_target_pairs={{1,0},{0,1},{3,2},{2,3},{5,4},{4,5},{7,6},{6,7},{9,8},{8,9},{11,10... | collective-permute-start | bytes 663560 | tf_op jit(solution)/shard_map/ppermute | solution.py:540
  14.2 15.3 %collective-permute-start.1 = (bf16[256,768]{1,0:T(8,128)(2,1)}, bf16[256,768]{1,0:T(8,128)(2,1)S(1)}, u32[]{:S(2)}, u32[]{:S(2)}) collective-permute-start(bf16[256,768]{1,0:T(8,128)(2,1)} %bitcast.105), channel_id=1, source_target_pairs={{16,0},{24,8},{0,16},{8,24},{17,1},{25,9},{1,17},{9,25},{18,2},{26... | collective-permute-start | bytes 1179656 | tf_op jit(solution)/shard_map/ppermute | solution.py:532
  27.2 11.1 %collective-permute-start.2 = (bf16[256,768]{1,0:T(8,128)(2,1)}, bf16[256,768]{1,0:T(8,128)(2,1)S(1)}, u32[]{:S(2)}, u32[]{:S(2)}) collective-permute-start(bf16[256,768]{1,0:T(8,128)(2,1)} %bitcast.106), channel_id=1, source_target_pairs={{24,0},{0,8},{8,16},{16,24},{25,1},{1,9},{9,17},{17,25},{26,2},{2,... | collective-permute-start | bytes 1179656 | tf_op jit(solution)/shard_map/ppermute | solution.py:532
  41.6 13.3 %collective-permute-start.11 = (bf16[192,768]{1,0:T(8,128)(2,1)}, bf16[192,768]{1,0:T(8,128)(2,1)S(1)}, u32[]{:S(2)}, u32[]{:S(2)}) collective-permute-start(bf16[192,768]{1,0:T(8,128)(2,1)} %param.26), channel_id=1, source_target_pairs={{0,4},{1,5},{10,14},{11,15},{20,16},{21,17},{30,26},{31,27}} | collective-permute-start | bytes 884744 | tf_op jit(solution)/shard_map/ppermute | solution.py:689
  42.9 15.2 %collective-permute-start.12 = (bf16[192,768]{1,0:T(8,128)(2,1)}, bf16[192,768]{1,0:T(8,128)(2,1)S(1)}, u32[]{:S(2)}, u32[]{:S(2)}) collective-permute-start(bf16[192,768]{1,0:T(8,128)(2,1)} %param.26), channel_id=1, source_target_pairs={{0,6},{1,7},{10,8},{11,9},{20,18},{21,19},{30,28},{31,29}} | collective-permute-start | bytes 884744 | tf_op jit(solution)/shard_map/ppermute | solution.py:689
  58.4 19.1 %collective-permute-start.13 = (bf16[1,192,768]{2,1,0:T(8,128)(2,1)S(1)}, bf16[1,192,768]{2,1,0:T(8,128)(2,1)S(1)}, u32[]{:S(2)}, u32[]{:S(2)}) collective-permute-start(bf16[1,192,768]{2,1,0:T(8,128)(2,1)S(1)} %bitcast.115), channel_id=1, source_target_pairs={{1,0},{0,1},{3,2},{2,3},{5,4},{4,5},{7,6},{6,7},{9,8},{8,9},{11,10... | collective-permute-start | bytes 884744 | tf_op jit(solution)/shard_map/ppermute | solution.py:540
  59.1 18.4 %collective-permute-start.17 = (bf16[256,768]{1,0:T(8,128)(2,1)S(1)}, bf16[256,768]{1,0:T(8,128)(2,1)S(1)}, u32[]{:S(2)}, u32[]{:S(2)}) collective-permute-start(bf16[256,768]{1,0:T(8,128)(2,1)S(1)} %bitcast.100), channel_id=1, source_target_pairs={{8,0},{16,8},{24,16},{0,24},{9,1},{17,9},{25,17},{1,25},{10,2},{18... | collective-permute-start | bytes 1179656 | tf_op jit(solution)/shard_map/ppermute | solution.py:532
  59.1 19.9 %collective-permute-start.18 = (bf16[256,768]{1,0:T(8,128)(2,1)S(1)}, bf16[256,768]{1,0:T(8,128)(2,1)S(1)}, u32[]{:S(2)}, u32[]{:S(2)}) collective-permute-start(bf16[256,768]{1,0:T(8,128)(2,1)S(1)} %bitcast.101), channel_id=1, source_target_pairs={{16,0},{24,8},{0,16},{8,24},{17,1},{25,9},{1,17},{9,25},{18,2},{26... | collective-permute-start | bytes 1179656 | tf_op jit(solution)/shard_map/ppermute | solution.py:532
  59.1 19.9 %collective-permute-start.19 = (bf16[256,768]{1,0:T(8,128)(2,1)S(1)}, bf16[256,768]{1,0:T(8,128)(2,1)S(1)}, u32[]{:S(2)}, u32[]{:S(2)}) collective-permute-start(bf16[256,768]{1,0:T(8,128)(2,1)S(1)} %bitcast.102), channel_id=1, source_target_pairs={{24,0},{0,8},{8,16},{16,24},{25,1},{1,9},{9,17},{17,25},{26,2},{2,... | collective-permute-start | bytes 1179656 | tf_op jit(solution)/shard_map/ppermute | solution.py:532
  133.1 12.3 %collective-permute-start.23 = (bf16[256,768]{1,0:T(8,128)(2,1)}, bf16[256,768]{1,0:T(8,128)(2,1)S(1)}, u32[]{:S(2)}, u32[]{:S(2)}) collective-permute-start(bf16[256,768]{1,0:T(8,128)(2,1)} %get-tuple-element.94), channel_id=1, source_target_pairs={{8,0},{16,8},{24,16},{0,24},{9,1},{17,9},{25,17},{1,25},{10,2},{18... | collective-permute-start | bytes 1179656 | tf_op jit(solution)/shard_map/ppermute | solution.py:532
  134.1 17.1 %collective-permute-start.24 = (bf16[256,768]{1,0:T(8,128)(2,1)}, bf16[256,768]{1,0:T(8,128)(2,1)S(1)}, u32[]{:S(2)}, u32[]{:S(2)}) collective-permute-start(bf16[256,768]{1,0:T(8,128)(2,1)} %get-tuple-element.95), channel_id=1, source_target_pairs={{16,0},{24,8},{0,16},{8,24},{17,1},{25,9},{1,17},{9,25},{18,2},{26... | collective-permute-start | bytes 1179656 | tf_op jit(solution)/shard_map/ppermute | solution.py:532
  135.4 19.4 %collective-permute-start.25 = (bf16[256,768]{1,0:T(8,128)(2,1)}, bf16[256,768]{1,0:T(8,128)(2,1)S(1)}, u32[]{:S(2)}, u32[]{:S(2)}) collective-permute-start(bf16[256,768]{1,0:T(8,128)(2,1)} %get-tuple-element.96), channel_id=1, source_target_pairs={{24,0},{0,8},{8,16},{16,24},{25,1},{1,9},{9,17},{17,25},{26,2},{2,... | collective-permute-start | bytes 1179656 | tf_op jit(solution)/shard_map/ppermute | solution.py:532
  141.6 20.7 %collective-permute-start.14 = (bf16[256,768]{1,0:T(8,128)(2,1)}, bf16[256,768]{1,0:T(8,128)(2,1)S(1)}, u32[]{:S(2)}, u32[]{:S(2)}) collective-permute-start(bf16[256,768]{1,0:T(8,128)(2,1)} %get-tuple-element.74), channel_id=1, source_target_pairs={{8,0},{16,8},{24,16},{0,24},{9,1},{17,9},{25,17},{1,25},{10,2},{18... | collective-permute-start | bytes 1179656 | tf_op jit(solution)/shard_map/ppermute | solution.py:532
  143.1 19.2 %collective-permute-start.15 = (bf16[256,768]{1,0:T(8,128)(2,1)}, bf16[256,768]{1,0:T(8,128)(2,1)S(1)}, u32[]{:S(2)}, u32[]{:S(2)}) collective-permute-start(bf16[256,768]{1,0:T(8,128)(2,1)} %get-tuple-element.75), channel_id=1, source_target_pairs={{16,0},{24,8},{0,16},{8,24},{17,1},{25,9},{1,17},{9,25},{18,2},{26... | collective-permute-start | bytes 1179656 | tf_op jit(solution)/shard_map/ppermute | solution.py:532
  145.4 23.7 %collective-permute-start.16 = (bf16[256,768]{1,0:T(8,128)(2,1)}, bf16[256,768]{1,0:T(8,128)(2,1)S(1)}, u32[]{:S(2)}, u32[]{:S(2)}) collective-permute-start(bf16[256,768]{1,0:T(8,128)(2,1)} %get-tuple-element.76), channel_id=1, source_target_pairs={{24,0},{0,8},{8,16},{16,24},{25,1},{1,9},{9,17},{17,25},{26,2},{2,... | collective-permute-start | bytes 1179656 | tf_op jit(solution)/shard_map/ppermute | solution.py:532
  151.2 19.5 %collective-permute-start.33 = (bf16[4,192,384]{2,1,0:T(8,128)(2,1)S(1)}, bf16[4,192,384]{2,1,0:T(8,128)(2,1)S(1)}, u32[]{:S(2)}, u32[]{:S(2)}) collective-permute-start(bf16[4,192,384]{2,1,0:T(8,128)(2,1)S(1)} %copy-done.34), channel_id=1, source_target_pairs={{1,0},{0,1},{3,2},{2,3},{5,4},{4,5},{7,6},{6,7},{9,8},{8,9},{11,10... | collective-permute-start | bytes 1769480 | tf_op jit(solution)/shard_map/ppermute | solution.py:540
  154.8 24.1 %collective-permute-start.26 = (bf16[400,768]{1,0:T(8,128)(2,1)S(1)}, bf16[400,768]{1,0:T(8,128)(2,1)S(1)}, u32[]{:S(2)}, u32[]{:S(2)}) collective-permute-start(bf16[400,768]{1,0:T(8,128)(2,1)S(1)} %copy-done.33), channel_id=1, source_target_pairs={{1,0},{0,1},{3,2},{2,3},{5,4},{4,5},{7,6},{6,7},{9,8},{8,9},{11,10... | collective-permute-start | bytes 1843208 | tf_op jit(solution)/shard_map/ppermute | solution.py:540
  176.0 22.8 %collective-permute-start.35 = (bf16[192,384]{1,0:T(8,128)(2,1)S(1)}, bf16[192,384]{1,0:T(8,128)(2,1)S(1)}, u32[]{:S(2)}, u32[]{:S(2)}) collective-permute-start(bf16[192,384]{1,0:T(8,128)(2,1)S(1)} %get-tuple-element.110), channel_id=1, source_target_pairs={{4,0},{5,1},{6,2},{7,3},{0,4},{1,5},{2,6},{3,7},{12,8},{13,9},{14,... | collective-permute-start | bytes 442376 | tf_op jit(solution)/shard_map/ppermute | solution.py:537
  177.0 21.8 %collective-permute-start.36 = (bf16[192,384]{1,0:T(8,128)(2,1)S(1)}, bf16[192,384]{1,0:T(8,128)(2,1)S(1)}, u32[]{:S(2)}, u32[]{:S(2)}) collective-permute-start(bf16[192,384]{1,0:T(8,128)(2,1)S(1)} %get-tuple-element.109), channel_id=1, source_target_pairs={{6,0},{7,1},{0,2},{1,3},{2,4},{3,5},{4,6},{5,7},{14,8},{15,9},{8,1... | collective-permute-start | bytes 442376 | tf_op jit(solution)/shard_map/ppermute | solution.py:537
  179.8 19.7 %collective-permute-start.27 = (bf16[112,768]{1,0:T(8,128)(2,1)S(1)}, bf16[112,768]{1,0:T(8,128)(2,1)S(1)}, u32[]{:S(2)}, u32[]{:S(2)}) collective-permute-start(bf16[112,768]{1,0:T(8,128)(2,1)S(1)} %get-tuple-element.126), channel_id=1, source_target_pairs={{2,0},{3,1},{4,2},{5,3},{6,4},{7,5},{0,6},{1,7},{10,8},{11,9},{12,... | collective-permute-start | bytes 516104 | tf_op jit(solution)/shard_map/ppermute | solution.py:537
  181.8 22.3 %collective-permute-start.28 = (bf16[112,768]{1,0:T(8,128)(2,1)S(1)}, bf16[112,768]{1,0:T(8,128)(2,1)S(1)}, u32[]{:S(2)}, u32[]{:S(2)}) collective-permute-start(bf16[112,768]{1,0:T(8,128)(2,1)S(1)} %get-tuple-element.127), channel_id=1, source_target_pairs={{4,0},{5,1},{6,2},{7,3},{0,4},{1,5},{2,6},{3,7},{12,8},{13,9},{14,... | collective-permute-start | bytes 516104 | tf_op jit(solution)/shard_map/ppermute | solution.py:537
  181.9 22.2 %collective-permute-start.29 = (bf16[112,768]{1,0:T(8,128)(2,1)S(1)}, bf16[112,768]{1,0:T(8,128)(2,1)S(1)}, u32[]{:S(2)}, u32[]{:S(2)}) collective-permute-start(bf16[112,768]{1,0:T(8,128)(2,1)S(1)} %get-tuple-element.128), channel_id=1, source_target_pairs={{6,0},{7,1},{0,2},{1,3},{2,4},{3,5},{4,6},{5,7},{14,8},{15,9},{8,1... | collective-permute-start | bytes 516104 | tf_op jit(solution)/shard_map/ppermute | solution.py:537
  198.9 15.4 %collective-permute-start.37 = (bf16[96,384]{1,0:T(8,128)(2,1)S(1)}, bf16[96,384]{1,0:T(8,128)(2,1)S(1)}, u32[]{:S(2)}, u32[]{:S(2)}) collective-permute-start(bf16[96,384]{1,0:T(8,128)(2,1)S(1)} %get-tuple-element.125), channel_id=1, source_target_pairs={{0,0},{1,8},{2,16},{3,24},{4,1},{5,9},{6,17},{7,25},{8,2},{9,10},{... | collective-permute-start | bytes 221192 | tf_op jit(solution)/shard_map/ppermute | solution.py:795
  204.2 13.1 %collective-permute-start.30 = (bf16[112,768]{1,0:T(8,128)(2,1)S(1)}, bf16[112,768]{1,0:T(8,128)(2,1)S(1)}, u32[]{:S(2)}, u32[]{:S(2)}) collective-permute-start(bf16[112,768]{1,0:T(8,128)(2,1)S(1)} %get-tuple-element.122), channel_id=1, source_target_pairs={{8,0},{16,8},{24,16},{0,24},{9,1},{17,9},{25,17},{1,25},{10,2},{18... | collective-permute-start | bytes 516104 | tf_op jit(solution)/shard_map/ppermute | solution.py:532
  206.1 12.2 %collective-permute-start.31 = (bf16[112,768]{1,0:T(8,128)(2,1)S(1)}, bf16[112,768]{1,0:T(8,128)(2,1)S(1)}, u32[]{:S(2)}, u32[]{:S(2)}) collective-permute-start(bf16[112,768]{1,0:T(8,128)(2,1)S(1)} %get-tuple-element.122), channel_id=1, source_target_pairs={{16,0},{24,8},{0,16},{8,24},{17,1},{25,9},{1,17},{9,25},{18,2},{26... | collective-permute-start | bytes 516104 | tf_op jit(solution)/shard_map/ppermute | solution.py:532
  214.3 25.7 %collective-permute-start.38 = (bf16[192,384]{1,0:T(8,128)(2,1)S(1)}, bf16[192,384]{1,0:T(8,128)(2,1)S(1)}, u32[]{:S(2)}, u32[]{:S(2)}) collective-permute-start(bf16[192,384]{1,0:T(8,128)(2,1)S(1)} %pad_maximum_fusion.8), channel_id=1, source_target_pairs={{8,0},{16,8},{24,16},{0,24},{9,1},{17,9},{25,17},{1,25},{10,2},{18... | collective-permute-start | bytes 442376 | tf_op jit(solution)/shard_map/ppermute | solution.py:532
  217.3 22.7 %collective-permute-start.39 = (bf16[192,384]{1,0:T(8,128)(2,1)S(1)}, bf16[192,384]{1,0:T(8,128)(2,1)S(1)}, u32[]{:S(2)}, u32[]{:S(2)}) collective-permute-start(bf16[192,384]{1,0:T(8,128)(2,1)S(1)} %pad_maximum_fusion.8), channel_id=1, source_target_pairs={{16,0},{24,8},{0,16},{8,24},{17,1},{25,9},{1,17},{9,25},{18,2},{26... | collective-permute-start | bytes 442376 | tf_op jit(solution)/shard_map/ppermute | solution.py:532
  217.4 22.7 %collective-permute-start.40 = (bf16[192,384]{1,0:T(8,128)(2,1)S(1)}, bf16[192,384]{1,0:T(8,128)(2,1)S(1)}, u32[]{:S(2)}, u32[]{:S(2)}) collective-permute-start(bf16[192,384]{1,0:T(8,128)(2,1)S(1)} %pad_maximum_fusion.8), channel_id=1, source_target_pairs={{24,0},{0,8},{8,16},{16,24},{25,1},{1,9},{9,17},{17,25},{26,2},{2,... | collective-permute-start | bytes 442376 | tf_op jit(solution)/shard_map/ppermute | solution.py:532
  (47 other events, 575.7 us)
